TPU v7x, 512 devices: a whole 4x4x16 slice. The times are simulated.
512 devices in a mesh: tm: 32 (over x_lo, z), height: 16 (over x_hi, y, core).
Axes of the slice: x: 4 (x_hi: 2, x_lo: 2; x = x_hi * 2 + x_lo), y: 4, z: 16, core: 2. Of those that a mesh axis runs over, the one named last changes fastest.
Arguments:
- query_vecs: bfloat16 [32, 16, 128, 1536], P('tm', 'height'), may hold values from -8 to 8
- key_vecs: bfloat16 [32, 16, 128, 1536], P('tm', 'height'), may hold values from -8 to 8
- value_vecs: bfloat16 [32, 16, 128, 1536], P('tm', 'height'), may hold values from -6 to 6
- grad_output: bfloat16 [32, 16, 128, 1536], P('tm', 'height'), may hold values from -6 to 6
- tile_window: int32 [12, 3], replicated, may hold values from 0 to 1, as said below
- neighbour_mask: int32 [12, 27], replicated, may hold values from 0 to 1, as said below
Outputs:
- attended: bfloat16 [32, 16, 128, 1536], P('tm', 'height')
- grad_query: bfloat16 [32, 16, 128, 1536], P('tm', 'height')
- grad_key: bfloat16 [32, 16, 128, 1536], P('tm', 'height')
- grad_value: bfloat16 [32, 16, 128, 1536], P('tm', 'height')
Inputs may be any that keep to these rules, and one draw needn't show every extreme that they name: `tile_window`: in each of the three columns exactly half of the 12 heads have 1 and the others 0. `neighbour_mask`: entry 13 (no offset) is 1 for every head.
All inputs are finite; a program needn't handle non-finite values.
Results may differ from a plain program's by a relative error of at most 0.025.
Values may be sent and summed in bfloat16 or wider, within the bound.
A program may use at most 64 MiB of HBM per device.

v0:
```python
import math

import jax
import jax.numpy as jnp
from jax import lax
from jax.sharding import PartitionSpec as P

TILE = 32


NEG_LARGE = -1e30


def with_halo(block, sides, width):
    for axis, dim in sides:
        count = lax.axis_size(axis)
        forward = [(i, i + 1) for i in range(count - 1)]
        backward = [(target, source) for source, target in forward]
        low = lax.ppermute(
            lax.slice_in_dim(block, block.shape[dim] - width, None, axis=dim), axis, forward
        )
        high = lax.ppermute(lax.slice_in_dim(block, 0, width, axis=dim), axis, backward)
        block = jnp.concatenate([low, block, high], axis=dim)
    return block


def contract(left, right, left_dim, right_dim):
    return lax.dot_general(
        left, right, (((left_dim,), (right_dim,)), ((), ())), preferred_element_type=jnp.float32
    )


def tile_coords(tile_count):
    counter = jnp.arange(9 * tile_count, dtype=jnp.int32)
    outer_t = counter // (3 * tile_count) - 1
    outer_h = counter // tile_count % 3 - 1
    outer_c = counter % tile_count
    inner_c = jnp.arange(tile_count, dtype=jnp.int32)
    return (outer_t, outer_h, outer_c, inner_c)


def pair_table(window_row, mask_row, step_t, step_h, step_w, inside):
    reach = (
        (jnp.abs(step_t) <= window_row[0])
        & (jnp.abs(step_h) <= window_row[1])
        & (jnp.abs(step_w) <= window_row[2])
    )
    offset = 9 * (step_t + 1) + 3 * (step_h + 1) + jnp.clip(step_w, -1, 1) + 1
    listed = jnp.sum(
        jnp.where(offset[..., None] == jnp.arange(27, dtype=jnp.int32), mask_row, 0), axis=-1
    )
    return reach & (listed > 0) & inside


def expand_table(tile_table):
    return jnp.repeat(jnp.repeat(tile_table, TILE, axis=0), TILE, axis=1)


def forward_tables(slab_len, time_pos, height_pos, time_count, height_count):
    tile_count = slab_len // TILE
    outer_t, outer_h, outer_c, inner_c = tile_coords(tile_count)
    inside = (
        (time_pos + outer_t >= 0)
        & (time_pos + outer_t < time_count)
        & (height_pos + outer_h >= 0)
        & (height_pos + outer_h < height_count)
    )
    step_t = jnp.broadcast_to(outer_t[None, :], (tile_count, 9 * tile_count))
    step_h = jnp.broadcast_to(outer_h[None, :], (tile_count, 9 * tile_count))
    step_w = outer_c[None, :] - inner_c[:, None]
    return (inside, step_t, step_h, step_w)


def head_forward(query_head, key_head, value_head, grad_head, allowed, scaling):
    scores = jnp.where(allowed, contract(query_head, key_head, 1, 1) * scaling, NEG_LARGE)
    highest = jnp.max(scores, axis=1, keepdims=True)
    log_sum = highest[:, 0] + jnp.log(jnp.sum(jnp.exp(scores - highest), axis=1))
    probs_high = jnp.exp(scores - log_sum[:, None])
    probs_low = probs_high.astype(jnp.bfloat16)
    out_head = contract(probs_low, value_head, 1, 0).astype(jnp.bfloat16)
    delta_row = jnp.sum(grad_head.astype(jnp.float32) * out_head.astype(jnp.float32), axis=1)
    grad_probs = contract(grad_head, value_head, 1, 1)
    grad_scores = (probs_high * (grad_probs - delta_row[:, None])).astype(jnp.bfloat16)
    grad_piece = (contract(grad_scores, key_head, 1, 0) * scaling).astype(jnp.bfloat16)
    return (out_head, grad_piece, log_sum, delta_row, probs_low, grad_scores)


def forward_block(
    query_loc,
    key_ext,
    value_ext,
    grad_loc,
    time_pos,
    height_pos,
    time_count,
    height_count,
    tile_window,
    neighbour_mask,
):
    slab_len, features = query_loc.shape
    head_count = tile_window.shape[0]
    head_width = features // head_count
    scaling = 1.0 / math.sqrt(head_width)
    inside, step_t, step_h, step_w = forward_tables(
        slab_len, time_pos, height_pos, time_count, height_count
    )

    def forward_one_head(number, carried):
        attended, grad_query, log_sums, deltas = carried
        allowed = expand_table(
            pair_table(
                tile_window[number], neighbour_mask[number], step_t, step_h, step_w, inside[None, :]
            )
        )
        start = number * head_width
        query_head = lax.dynamic_slice_in_dim(query_loc, start, head_width, 1)
        key_head = lax.dynamic_slice_in_dim(key_ext, start, head_width, 1)
        value_head = lax.dynamic_slice_in_dim(value_ext, start, head_width, 1)
        grad_head = lax.dynamic_slice_in_dim(grad_loc, start, head_width, 1)
        out_head, grad_piece, log_sum, delta_row, probs_low, grad_scores = head_forward(
            query_head, key_head, value_head, grad_head, allowed, scaling
        )
        attended = lax.dynamic_update_slice_in_dim(attended, out_head, start, 1)
        grad_query = lax.dynamic_update_slice_in_dim(grad_query, grad_piece, start, 1)
        log_sums = lax.dynamic_update_slice_in_dim(log_sums, log_sum[None, :], number, 0)
        deltas = lax.dynamic_update_slice_in_dim(deltas, delta_row[None, :], number, 0)
        return (attended, grad_query, log_sums, deltas)

    initial = (
        jnp.zeros((slab_len, features), jnp.bfloat16),
        jnp.zeros((slab_len, features), jnp.bfloat16),
        jnp.zeros((head_count, slab_len), jnp.float32),
        jnp.zeros((head_count, slab_len), jnp.float32),
    )
    return lax.fori_loop(0, head_count, forward_one_head, initial)


def backward_block(
    query_ext,
    grad_ext,
    sums_ext,
    deltas_ext,
    key_loc,
    value_loc,
    time_pos,
    height_pos,
    time_count,
    height_count,
    tile_window,
    neighbour_mask,
):
    slab_len, features = key_loc.shape
    head_count = tile_window.shape[0]
    head_width = features // head_count
    tile_count = slab_len // TILE
    scaling = 1.0 / math.sqrt(head_width)
    outer_t, outer_h, outer_c, inner_c = tile_coords(tile_count)
    inside = (
        (time_pos + outer_t >= 0)
        & (time_pos + outer_t < time_count)
        & (height_pos + outer_h >= 0)
        & (height_pos + outer_h < height_count)
    )
    step_t = jnp.broadcast_to(-outer_t[:, None], (9 * tile_count, tile_count))
    step_h = jnp.broadcast_to(-outer_h[:, None], (9 * tile_count, tile_count))
    step_w = inner_c[None, :] - outer_c[:, None]

    def backward_one_head(number, carried):
        grad_key, grad_value = carried
        allowed = expand_table(
            pair_table(
                tile_window[number], neighbour_mask[number], step_t, step_h, step_w, inside[:, None]
            )
        )
        start = number * head_width
        query_head = lax.dynamic_slice_in_dim(query_ext, start, head_width, 1)
        grad_head = lax.dynamic_slice_in_dim(grad_ext, start, head_width, 1)
        key_head = lax.dynamic_slice_in_dim(key_loc, start, head_width, 1)
        value_head = lax.dynamic_slice_in_dim(value_loc, start, head_width, 1)
        sum_row = lax.dynamic_index_in_dim(sums_ext, number, 0, keepdims=False)
        delta_row = lax.dynamic_index_in_dim(deltas_ext, number, 0, keepdims=False)
        scores = jnp.where(allowed, contract(query_head, key_head, 1, 1) * scaling, NEG_LARGE)
        probs_high = jnp.exp(scores - sum_row[:, None])
        probs_low = probs_high.astype(jnp.bfloat16)
        value_piece = contract(probs_low, grad_head, 0, 0).astype(jnp.bfloat16)
        grad_probs = contract(grad_head, value_head, 1, 1)
        grad_scores = (probs_high * (grad_probs - delta_row[:, None])).astype(jnp.bfloat16)
        key_piece = (contract(grad_scores, query_head, 0, 0) * scaling).astype(jnp.bfloat16)
        grad_key = lax.dynamic_update_slice_in_dim(grad_key, key_piece, start, 1)
        grad_value = lax.dynamic_update_slice_in_dim(grad_value, value_piece, start, 1)
        return (grad_key, grad_value)

    initial = (
        jnp.zeros((slab_len, features), jnp.bfloat16),
        jnp.zeros((slab_len, features), jnp.bfloat16),
    )
    return lax.fori_loop(0, head_count, backward_one_head, initial)


def on_device(query_vecs, key_vecs, value_vecs, grad_output, tile_window, neighbour_mask):
    time_pos = lax.axis_index("tm")
    height_pos = lax.axis_index("height")
    time_count = lax.axis_size("tm")
    height_count = lax.axis_size("height")
    slab_len = query_vecs.shape[2]
    features = query_vecs.shape[3]
    head_count = tile_window.shape[0]
    key_ext, value_ext = (
        with_halo(key_vecs, (("tm", 0), ("height", 1)), 1),
        with_halo(value_vecs, (("tm", 0), ("height", 1)), 1),
    )
    query_loc = query_vecs.reshape(slab_len, features)
    grad_loc = grad_output.reshape(slab_len, features)
    out_shape = (1, 1, slab_len, features)
    attended, grad_query, log_sums, deltas = forward_block(
        query_loc,
        key_ext.reshape(9 * slab_len, features),
        value_ext.reshape(9 * slab_len, features),
        grad_loc,
        time_pos,
        height_pos,
        time_count,
        height_count,
        tile_window,
        neighbour_mask,
    )
    sums_ext, deltas_ext = (
        with_halo(log_sums[None, None], (("tm", 0), ("height", 1)), 1),
        with_halo(deltas[None, None], (("tm", 0), ("height", 1)), 1),
    )
    query_ext, grad_ext = (
        with_halo(query_vecs, (("tm", 0), ("height", 1)), 1),
        with_halo(grad_output, (("tm", 0), ("height", 1)), 1),
    )
    sums_rows = sums_ext.transpose(2, 0, 1, 3).reshape(head_count, 9 * slab_len)
    deltas_rows = deltas_ext.transpose(2, 0, 1, 3).reshape(head_count, 9 * slab_len)
    grad_key, grad_value = backward_block(
        query_ext.reshape(9 * slab_len, features),
        grad_ext.reshape(9 * slab_len, features),
        sums_rows,
        deltas_rows,
        key_vecs.reshape(slab_len, features),
        value_vecs.reshape(slab_len, features),
        time_pos,
        height_pos,
        time_count,
        height_count,
        tile_window,
        neighbour_mask,
    )
    return (
        attended.reshape(out_shape),
        grad_query.reshape(out_shape),
        grad_key.reshape(out_shape),
        grad_value.reshape(out_shape),
    )


def solution(mesh):
    in_specs = (
        P("tm", "height", None, None),
        P("tm", "height", None, None),
        P("tm", "height", None, None),
        P("tm", "height", None, None),
        P(),
        P(),
    )
    out_specs = (
        P("tm", "height", None, None),
        P("tm", "height", None, None),
        P("tm", "height", None, None),
        P("tm", "height", None, None),
    )
    return jax.shard_map(
        on_device, mesh=mesh, in_specs=in_specs, out_specs=out_specs, check_vma=False
    )
```

profile of v0, /device:TPU:27, one launch (start us, length us, event | category | flops | bytes accessed | tf_op | source)
XLA Modules:
  0.0 351.5 jit_solution(9639511444190987273)
XLA Ops:
  0.6 3.7 %collective-permute-start.4 = (bf16[1,1,128,1536]{3,2,1,0:T(8,128)(2,1)}, bf16[1,1,128,1536]{3,2,1,0:T(8,128)(2,1)S(1)}, u32[]{:S(2)}, u32[]{:S(2)}) collective-permute-start(bf16[1,1,128,1536]{3,2,1,0:T(8,128)(2,1)} %param.12), channel_id=1, source_target_pairs={{0,16},{16,32},{32,48},{48,64},{64,80},{80,96},{96,112},{112,128},... | collective-permute-start | bytes 1179656 | tf_op jit(solution)/shard_map/ppermute | solution.py:19
  4.3 9.5 %collective-permute-start.5 = (bf16[1,1,128,1536]{3,2,1,0:T(8,128)(2,1)}, bf16[1,1,128,1536]{3,2,1,0:T(8,128)(2,1)S(1)}, u32[]{:S(2)}, u32[]{:S(2)}) collective-permute-start(bf16[1,1,128,1536]{3,2,1,0:T(8,128)(2,1)} %param.12), channel_id=1, source_target_pairs={{16,0},{32,16},{48,32},{64,48},{80,64},{96,80},{112,96},{128,112},... | collective-permute-start | bytes 1179656 | tf_op jit(solution)/shard_map/ppermute | solution.py:22
  13.8 1.9 collective-permute-start
  15.7 5.5 %collective-permute-start.1 = (bf16[1,1,128,1536]{3,2,1,0:T(8,128)(2,1)}, bf16[1,1,128,1536]{3,2,1,0:T(8,128)(2,1)S(1)}, u32[]{:S(2)}, u32[]{:S(2)}) collective-permute-start(bf16[1,1,128,1536]{3,2,1,0:T(8,128)(2,1)} %param.11), channel_id=1, source_target_pairs={{16,0},{32,16},{48,32},{64,48},{80,64},{96,80},{112,96},{128,112},... | collective-permute-start | bytes 1179656 | tf_op jit(solution)/shard_map/ppermute | solution.py:22
  21.2 1.9 collective-permute-start.16
  24.5 5.5 %collective-permute-start.17 = (bf16[1,1,128,1536]{3,2,1,0:T(8,128)(2,1)}, bf16[1,1,128,1536]{3,2,1,0:T(8,128)(2,1)S(1)}, u32[]{:S(2)}, u32[]{:S(2)}) collective-permute-start(bf16[1,1,128,1536]{3,2,1,0:T(8,128)(2,1)} %param.13), channel_id=1, source_target_pairs={{16,0},{32,16},{48,32},{64,48},{80,64},{96,80},{112,96},{128,112},... | collective-permute-start | bytes 1179656 | tf_op jit(solution)/shard_map/ppermute | solution.py:22
  30.1 2.1 collective-permute-start.8
  32.2 5.7 %collective-permute-start.6 = (bf16[3,1,128,1536]{3,2,1,0:T(8,128)(2,1)S(1)}, bf16[3,1,128,1536]{3,2,1,0:T(8,128)(2,1)S(1)}, u32[]{:S(2)}, u32[]{:S(2)}) collective-permute-start(bf16[3,1,128,1536]{3,2,1,0:T(8,128)(2,1)S(1)} %constant_dynamic-update-slice_fusion.4), channel_id=1, source_target_pairs={{0,1},{1,2},{2,3},{3,4},{4,5},{5,6},{6,7},{7,8},{8,9},{9,10},{10,1... | collective-permute-start | bytes 3538952 | tf_op jit(solution)/shard_map/ppermute | solution.py:19
  38.0 2.1 collective-permute-start.7
  40.1 7.3 %collective-permute-start.2 = (bf16[3,1,128,1536]{3,2,1,0:T(8,128)(2,1)S(1)}, bf16[3,1,128,1536]{3,2,1,0:T(8,128)(2,1)S(1)}, u32[]{:S(2)}, u32[]{:S(2)}) collective-permute-start(bf16[3,1,128,1536]{3,2,1,0:T(8,128)(2,1)S(1)} %constant_dynamic-update-slice_fusion.1), channel_id=1, source_target_pairs={{0,1},{1,2},{2,3},{3,4},{4,5},{5,6},{6,7},{7,8},{8,9},{9,10},{10,1... | collective-permute-start | bytes 3538952 | tf_op jit(solution)/shard_map/ppermute | solution.py:19
  47.4 2.0 collective-permute-start.3
  49.5 6.3 %collective-permute-start.9 = (bf16[1,1,128,1536]{3,2,1,0:T(8,128)(2,1)}, bf16[1,1,128,1536]{3,2,1,0:T(8,128)(2,1)S(1)}, u32[]{:S(2)}, u32[]{:S(2)}) collective-permute-start(bf16[1,1,128,1536]{3,2,1,0:T(8,128)(2,1)} %param.10), channel_id=1, source_target_pairs={{16,0},{32,16},{48,32},{64,48},{80,64},{96,80},{112,96},{128,112},... | collective-permute-start | bytes 1179656 | tf_op jit(solution)/shard_map/ppermute | solution.py:22
  56.9 5.6 %collective-permute-done.9 = bf16[1,1,128,1536]{3,2,1,0:T(8,128)(2,1)S(1)} collective-permute-done((bf16[1,1,128,1536]{3,2,1,0:T(8,128)(2,1)}, bf16[1,1,128,1536]{3,2,1,0:T(8,128)(2,1)S(1)}, u32[]{:S(2)}, u32[]{:S(2)}) %collective-permute-start.9) | collective-permute-done | bytes 393248 | tf_op jit(solution)/shard_map/ppermute | solution.py:22
  62.5 5.9 %collective-permute-start.18 = (bf16[3,1,128,1536]{3,2,1,0:T(8,128)(2,1)S(1)}, bf16[3,1,128,1536]{3,2,1,0:T(8,128)(2,1)}, u32[]{:S(2)}, u32[]{:S(2)}) collective-permute-start(bf16[3,1,128,1536]{3,2,1,0:T(8,128)(2,1)S(1)} %constant_dynamic-update-slice_fusion.10), channel_id=1, source_target_pairs={{0,1},{1,2},{2,3},{3,4},{4,5},{5,6},{6,7},{7,8},{8,9},{9,10},{10,1... | collective-permute-start | bytes 3538952 | tf_op jit(solution)/shard_map/ppermute | solution.py:19
  68.4 1.9 collective-permute-start.19
  70.3 7.3 %collective-permute-start.10 = (bf16[3,1,128,1536]{3,2,1,0:T(8,128)(2,1)S(1)}, bf16[3,1,128,1536]{3,2,1,0:T(8,128)(2,1)}, u32[]{:S(2)}, u32[]{:S(2)}) collective-permute-start(bf16[3,1,128,1536]{3,2,1,0:T(8,128)(2,1)S(1)} %constant_dynamic-update-slice_fusion.7), channel_id=1, source_target_pairs={{0,1},{1,2},{2,3},{3,4},{4,5},{5,6},{6,7},{7,8},{8,9},{9,10},{10,1... | collective-permute-start | bytes 3538952 | tf_op jit(solution)/shard_map/ppermute | solution.py:19
  77.6 2.0 pad_maximum_fusion.1
  79.6 2.0 collective-permute-start.11
  81.6 2.0 pad_maximum_fusion
  85.2 118.7 %while.40 = (s32[]{:T(128)}, bf16[128,1536]{1,0:T(8,128)(2,1)}, bf16[128,1536]{1,0:T(8,128)(2,1)}, f32[12,128]{1,0:T(8,128)S(1)}, f32[12,128]{1,0:T(8,128)S(1)},...) while((s32[]{:T(128)}, bf16[128,1536]{1,0:T(8,128)(2,1)}, ...), condition=%wide.region_5.6_spmd.clone.clone, body=%wide.region_0.5_spmd.clone.clone.sunk | while | flops 152745904 | bytes 4458207 | solution.py:135
  92.2 2.1 fusion.143
  102.0 2.1 fusion.143
  111.9 2.1 fusion.143
  121.8 2.1 fusion.143
  131.7 2.1 fusion.143
  141.6 2.1 fusion.143
  151.5 2.1 fusion.143
  161.4 2.1 fusion.143
  171.3 2.1 fusion.143
  181.2 2.1 fusion.143
  191.0 2.1 fusion.143
  200.9 2.1 fusion.143
  203.8 1.9 collective-permute-start.20
  205.8 6.8 %collective-permute-start.21 = (f32[1,1,12,128]{3,2,1,0:T(8,128)S(1)}, f32[1,1,12,128]{3,2,1,0:T(8,128)S(1)}, u32[]{:S(2)}, u32[]{:S(2)}) collective-permute-start(f32[1,1,12,128]{3,2,1,0:T(8,128)S(1)} %bitcast.80), channel_id=1, source_target_pairs={{16,0},{32,16},{48,32},{64,48},{80,64},{96,80},{112,96},{128,112},... | collective-permute-start | bytes 18440 | tf_op jit(solution)/shard_map/ppermute | solution.py:22
  212.6 1.9 collective-permute-start.12
  214.5 3.2 pad_maximum_fusion.3
  217.7 5.5 %collective-permute-start.13 = (f32[1,1,12,128]{3,2,1,0:T(8,128)S(1)}, f32[1,1,12,128]{3,2,1,0:T(8,128)S(1)}, u32[]{:S(2)}, u32[]{:S(2)}) collective-permute-start(f32[1,1,12,128]{3,2,1,0:T(8,128)S(1)} %bitcast.76), channel_id=1, source_target_pairs={{16,0},{32,16},{48,32},{64,48},{80,64},{96,80},{112,96},{128,112},... | collective-permute-start | bytes 18440 | tf_op jit(solution)/shard_map/ppermute | solution.py:22
  223.2 3.2 pad_maximum_fusion.2
  226.4 7.5 %collective-permute-start.22 = (f32[3,1,12,128]{3,2,1,0:T(8,128)S(1)}, f32[3,1,12,128]{3,2,1,0:T(8,128)S(1)}, u32[]{:S(2)}, u32[]{:S(2)}) collective-permute-start(f32[3,1,12,128]{3,2,1,0:T(8,128)S(1)} %pad_maximum_fusion.5), channel_id=1, source_target_pairs={{0,1},{1,2},{2,3},{3,4},{4,5},{5,6},{6,7},{7,8},{8,9},{9,10},{10,1... | collective-permute-start | bytes 55304 | tf_op jit(solution)/shard_map/ppermute | solution.py:19
  233.9 1.9 collective-permute-start.23
  235.9 7.3 %collective-permute-start.14 = (f32[3,1,12,128]{3,2,1,0:T(8,128)S(1)}, f32[3,1,12,128]{3,2,1,0:T(8,128)S(1)}, u32[]{:S(2)}, u32[]{:S(2)}) collective-permute-start(f32[3,1,12,128]{3,2,1,0:T(8,128)S(1)} %pad_maximum_fusion.4), channel_id=1, source_target_pairs={{0,1},{1,2},{2,3},{3,4},{4,5},{5,6},{6,7},{7,8},{8,9},{9,10},{10,1... | collective-permute-start | bytes 55304 | tf_op jit(solution)/shard_map/ppermute | solution.py:19
  243.2 1.9 collective-permute-start.15
  245.2 6.7 %collective-permute-done.15 = f32[3,1,12,128]{3,2,1,0:T(8,128)S(1)} collective-permute-done((f32[3,1,12,128]{3,2,1,0:T(8,128)S(1)}, f32[3,1,12,128]{3,2,1,0:T(8,128)S(1)}, u32[]{:S(2)}, u32[]{:S(2)}) %collective-permute-start.15) | collective-permute-done | bytes 18464 | tf_op jit(solution)/shard_map/ppermute | solution.py:22
  252.1 98.5 %while.41 = (s32[]{:T(128)}, bf16[128,1536]{1,0:T(8,128)(2,1)S(1)}, bf16[128,1536]{1,0:T(8,128)(2,1)S(1)}, s32[12,3]{0,1:T(4,128)S(1)}, s32[12,27]{1,0:T(8,128)}...) while((s32[]{:T(128)}, bf16[128,1536]{1,0:T(8,128)(2,1)S(1)}, ...), condition=%wide.region_8.9_spmd.clone.clone, body=%wide.region_6.8_spmd.clone.clone.sunk | while | flops 152090800 | bytes 3728311 | solution.py:197
  275.1 1.6 fusion.156
  283.3 1.6 fusion.156
  299.7 1.6 fusion.156
  324.3 1.6 fusion.156
  (506 shorter events, 188.8 us)
Async XLA Ops:
  0.6 29.4 %copy-start.2 = (bf16[1,1,128,1536]{3,2,1,0:T(8,128)(2,1)S(1)}, bf16[1,1,128,1536]{3,2,1,0:T(8,128)(2,1)}, u32[]{:S(2)}) copy-start(bf16[1,1,128,1536]{3,2,1,0:T(8,128)(2,1)} %param.12) | copy-start | bytes 1179652
  0.6 23.9 %collective-permute-start.4 = (bf16[1,1,128,1536]{3,2,1,0:T(8,128)(2,1)}, bf16[1,1,128,1536]{3,2,1,0:T(8,128)(2,1)S(1)}, u32[]{:S(2)}, u32[]{:S(2)}) collective-permute-start(bf16[1,1,128,1536]{3,2,1,0:T(8,128)(2,1)} %param.12), channel_id=1, source_target_pairs={{0,16},{16,32},{32,48},{48,64},{64,80},{80,96},{96,112},{112,128},... | collective-permute-start | bytes 1179656 | tf_op jit(solution)/shard_map/ppermute | solution.py:19
  4.3 25.8 %collective-permute-start.5 = (bf16[1,1,128,1536]{3,2,1,0:T(8,128)(2,1)}, bf16[1,1,128,1536]{3,2,1,0:T(8,128)(2,1)S(1)}, u32[]{:S(2)}, u32[]{:S(2)}) collective-permute-start(bf16[1,1,128,1536]{3,2,1,0:T(8,128)(2,1)} %param.12), channel_id=1, source_target_pairs={{16,0},{32,16},{48,32},{64,48},{80,64},{96,80},{112,96},{128,112},... | collective-permute-start | bytes 1179656 | tf_op jit(solution)/shard_map/ppermute | solution.py:22
  13.8 18.4 %collective-permute-start = (bf16[1,1,128,1536]{3,2,1,0:T(8,128)(2,1)}, bf16[1,1,128,1536]{3,2,1,0:T(8,128)(2,1)S(1)}, u32[]{:S(2)}, u32[]{:S(2)}) collective-permute-start(bf16[1,1,128,1536]{3,2,1,0:T(8,128)(2,1)} %param.11), channel_id=1, source_target_pairs={{0,16},{16,32},{32,48},{48,64},{64,80},{80,96},{96,112},{112,128},... | collective-permute-start | bytes 1179656 | tf_op jit(solution)/shard_map/ppermute | solution.py:19
  15.7 22.2 %collective-permute-start.1 = (bf16[1,1,128,1536]{3,2,1,0:T(8,128)(2,1)}, bf16[1,1,128,1536]{3,2,1,0:T(8,128)(2,1)S(1)}, u32[]{:S(2)}, u32[]{:S(2)}) collective-permute-start(bf16[1,1,128,1536]{3,2,1,0:T(8,128)(2,1)} %param.11), channel_id=1, source_target_pairs={{16,0},{32,16},{48,32},{64,48},{80,64},{96,80},{112,96},{128,112},... | collective-permute-start | bytes 1179656 | tf_op jit(solution)/shard_map/ppermute | solution.py:22
  21.2 18.9 %collective-permute-start.16 = (bf16[1,1,128,1536]{3,2,1,0:T(8,128)(2,1)}, bf16[1,1,128,1536]{3,2,1,0:T(8,128)(2,1)S(1)}, u32[]{:S(2)}, u32[]{:S(2)}) collective-permute-start(bf16[1,1,128,1536]{3,2,1,0:T(8,128)(2,1)} %param.13), channel_id=1, source_target_pairs={{0,16},{16,32},{32,48},{48,64},{64,80},{80,96},{96,112},{112,128},... | collective-permute-start | bytes 1179656 | tf_op jit(solution)/shard_map/ppermute | solution.py:19
  24.5 24.9 %collective-permute-start.17 = (bf16[1,1,128,1536]{3,2,1,0:T(8,128)(2,1)}, bf16[1,1,128,1536]{3,2,1,0:T(8,128)(2,1)S(1)}, u32[]{:S(2)}, u32[]{:S(2)}) collective-permute-start(bf16[1,1,128,1536]{3,2,1,0:T(8,128)(2,1)} %param.13), channel_id=1, source_target_pairs={{16,0},{32,16},{48,32},{64,48},{80,64},{96,80},{112,96},{128,112},... | collective-permute-start | bytes 1179656 | tf_op jit(solution)/shard_map/ppermute | solution.py:22
  30.0 7.9 %copy-start.1 = (bf16[1,1,128,1536]{3,2,1,0:T(8,128)(2,1)S(1)}, bf16[1,1,128,1536]{3,2,1,0:T(8,128)(2,1)}, u32[]{:S(2)}) copy-start(bf16[1,1,128,1536]{3,2,1,0:T(8,128)(2,1)} %param.11) | copy-start | bytes 1179652
  30.1 17.3 %collective-permute-start.8 = (bf16[1,1,128,1536]{3,2,1,0:T(8,128)(2,1)}, bf16[1,1,128,1536]{3,2,1,0:T(8,128)(2,1)S(1)}, u32[]{:S(2)}, u32[]{:S(2)}) collective-permute-start(bf16[1,1,128,1536]{3,2,1,0:T(8,128)(2,1)} %param.10), channel_id=1, source_target_pairs={{0,16},{16,32},{32,48},{48,64},{64,80},{80,96},{96,112},{112,128},... | collective-permute-start | bytes 1179656 | tf_op jit(solution)/shard_map/ppermute | solution.py:19
  32.2 36.2 %collective-permute-start.6 = (bf16[3,1,128,1536]{3,2,1,0:T(8,128)(2,1)S(1)}, bf16[3,1,128,1536]{3,2,1,0:T(8,128)(2,1)S(1)}, u32[]{:S(2)}, u32[]{:S(2)}) collective-permute-start(bf16[3,1,128,1536]{3,2,1,0:T(8,128)(2,1)S(1)} %constant_dynamic-update-slice_fusion.4), channel_id=1, source_target_pairs={{0,1},{1,2},{2,3},{3,4},{4,5},{5,6},{6,7},{7,8},{8,9},{9,10},{10,1... | collective-permute-start | bytes 3538952 | tf_op jit(solution)/shard_map/ppermute | solution.py:19
  37.9 9.5 %copy-start = (bf16[1,1,128,1536]{3,2,1,0:T(8,128)(2,1)S(1)}, bf16[1,1,128,1536]{3,2,1,0:T(8,128)(2,1)}, u32[]{:S(2)}) copy-start(bf16[1,1,128,1536]{3,2,1,0:T(8,128)(2,1)} %param.13) | copy-start | bytes 1179652
  38.0 32.3 %collective-permute-start.7 = (bf16[3,1,128,1536]{3,2,1,0:T(8,128)(2,1)S(1)}, bf16[3,1,128,1536]{3,2,1,0:T(8,128)(2,1)S(1)}, u32[]{:S(2)}, u32[]{:S(2)}) collective-permute-start(bf16[3,1,128,1536]{3,2,1,0:T(8,128)(2,1)S(1)} %constant_dynamic-update-slice_fusion.4), channel_id=1, source_target_pairs={{1,0},{2,1},{3,2},{4,3},{5,4},{6,5},{7,6},{8,7},{9,8},{10,9},{11,1... | collective-permute-start | bytes 3538952 | tf_op jit(solution)/shard_map/ppermute | solution.py:22
  40.1 39.5 %collective-permute-start.2 = (bf16[3,1,128,1536]{3,2,1,0:T(8,128)(2,1)S(1)}, bf16[3,1,128,1536]{3,2,1,0:T(8,128)(2,1)S(1)}, u32[]{:S(2)}, u32[]{:S(2)}) collective-permute-start(bf16[3,1,128,1536]{3,2,1,0:T(8,128)(2,1)S(1)} %constant_dynamic-update-slice_fusion.1), channel_id=1, source_target_pairs={{0,1},{1,2},{2,3},{3,4},{4,5},{5,6},{6,7},{7,8},{8,9},{9,10},{10,1... | collective-permute-start | bytes 3538952 | tf_op jit(solution)/shard_map/ppermute | solution.py:19
  47.4 34.2 %collective-permute-start.3 = (bf16[3,1,128,1536]{3,2,1,0:T(8,128)(2,1)S(1)}, bf16[3,1,128,1536]{3,2,1,0:T(8,128)(2,1)S(1)}, u32[]{:S(2)}, u32[]{:S(2)}) collective-permute-start(bf16[3,1,128,1536]{3,2,1,0:T(8,128)(2,1)S(1)} %constant_dynamic-update-slice_fusion.1), channel_id=1, source_target_pairs={{1,0},{2,1},{3,2},{4,3},{5,4},{6,5},{7,6},{8,7},{9,8},{10,9},{11,1... | collective-permute-start | bytes 3538952 | tf_op jit(solution)/shard_map/ppermute | solution.py:22
  49.5 13.0 %collective-permute-start.9 = (bf16[1,1,128,1536]{3,2,1,0:T(8,128)(2,1)}, bf16[1,1,128,1536]{3,2,1,0:T(8,128)(2,1)S(1)}, u32[]{:S(2)}, u32[]{:S(2)}) collective-permute-start(bf16[1,1,128,1536]{3,2,1,0:T(8,128)(2,1)} %param.10), channel_id=1, source_target_pairs={{16,0},{32,16},{48,32},{64,48},{80,64},{96,80},{112,96},{128,112},... | collective-permute-start | bytes 1179656 | tf_op jit(solution)/shard_map/ppermute | solution.py:22
  62.5 143.3 %collective-permute-start.18 = (bf16[3,1,128,1536]{3,2,1,0:T(8,128)(2,1)S(1)}, bf16[3,1,128,1536]{3,2,1,0:T(8,128)(2,1)}, u32[]{:S(2)}, u32[]{:S(2)}) collective-permute-start(bf16[3,1,128,1536]{3,2,1,0:T(8,128)(2,1)S(1)} %constant_dynamic-update-slice_fusion.10), channel_id=1, source_target_pairs={{0,1},{1,2},{2,3},{3,4},{4,5},{5,6},{6,7},{7,8},{8,9},{9,10},{10,1... | collective-permute-start | bytes 3538952 | tf_op jit(solution)/shard_map/ppermute | solution.py:19
  68.4 144.2 %collective-permute-start.19 = (bf16[3,1,128,1536]{3,2,1,0:T(8,128)(2,1)S(1)}, bf16[3,1,128,1536]{3,2,1,0:T(8,128)(2,1)}, u32[]{:S(2)}, u32[]{:S(2)}) collective-permute-start(bf16[3,1,128,1536]{3,2,1,0:T(8,128)(2,1)S(1)} %constant_dynamic-update-slice_fusion.10), channel_id=1, source_target_pairs={{1,0},{2,1},{3,2},{4,3},{5,4},{6,5},{7,6},{8,7},{9,8},{10,9},{11,1... | collective-permute-start | bytes 3538952 | tf_op jit(solution)/shard_map/ppermute | solution.py:22
  70.3 147.4 %collective-permute-start.10 = (bf16[3,1,128,1536]{3,2,1,0:T(8,128)(2,1)S(1)}, bf16[3,1,128,1536]{3,2,1,0:T(8,128)(2,1)}, u32[]{:S(2)}, u32[]{:S(2)}) collective-permute-start(bf16[3,1,128,1536]{3,2,1,0:T(8,128)(2,1)S(1)} %constant_dynamic-update-slice_fusion.7), channel_id=1, source_target_pairs={{0,1},{1,2},{2,3},{3,4},{4,5},{5,6},{6,7},{7,8},{8,9},{9,10},{10,1... | collective-permute-start | bytes 3538952 | tf_op jit(solution)/shard_map/ppermute | solution.py:19
  79.6 5.6 %copy-start.5 = (s32[12,3]{0,1:T(4,128)S(1)}, s32[12,3]{0,1:T(4,128)}, u32[]{:S(2)}) copy-start(s32[12,3]{0,1:T(4,128)} %param.14) | copy-start | bytes 436
  79.6 143.6 %collective-permute-start.11 = (bf16[3,1,128,1536]{3,2,1,0:T(8,128)(2,1)S(1)}, bf16[3,1,128,1536]{3,2,1,0:T(8,128)(2,1)}, u32[]{:S(2)}, u32[]{:S(2)}) collective-permute-start(bf16[3,1,128,1536]{3,2,1,0:T(8,128)(2,1)S(1)} %constant_dynamic-update-slice_fusion.7), channel_id=1, source_target_pairs={{1,0},{2,1},{3,2},{4,3},{5,4},{6,5},{7,6},{8,7},{9,8},{10,9},{11,1... | collective-permute-start | bytes 3538952 | tf_op jit(solution)/shard_map/ppermute | solution.py:22
  203.8 22.6 %collective-permute-start.20 = (f32[1,1,12,128]{3,2,1,0:T(8,128)S(1)}, f32[1,1,12,128]{3,2,1,0:T(8,128)S(1)}, u32[]{:S(2)}, u32[]{:S(2)}) collective-permute-start(f32[1,1,12,128]{3,2,1,0:T(8,128)S(1)} %bitcast.79), channel_id=1, source_target_pairs={{0,16},{16,32},{32,48},{48,64},{64,80},{80,96},{96,112},{112,128},... | collective-permute-start | bytes 18440 | tf_op jit(solution)/shard_map/ppermute | solution.py:19
  205.8 20.6 %collective-permute-start.21 = (f32[1,1,12,128]{3,2,1,0:T(8,128)S(1)}, f32[1,1,12,128]{3,2,1,0:T(8,128)S(1)}, u32[]{:S(2)}, u32[]{:S(2)}) collective-permute-start(f32[1,1,12,128]{3,2,1,0:T(8,128)S(1)} %bitcast.80), channel_id=1, source_target_pairs={{16,0},{32,16},{48,32},{64,48},{80,64},{96,80},{112,96},{128,112},... | collective-permute-start | bytes 18440 | tf_op jit(solution)/shard_map/ppermute | solution.py:22
  212.6 23.3 %collective-permute-start.12 = (f32[1,1,12,128]{3,2,1,0:T(8,128)S(1)}, f32[1,1,12,128]{3,2,1,0:T(8,128)S(1)}, u32[]{:S(2)}, u32[]{:S(2)}) collective-permute-start(f32[1,1,12,128]{3,2,1,0:T(8,128)S(1)} %bitcast.75), channel_id=1, source_target_pairs={{0,16},{16,32},{32,48},{48,64},{64,80},{80,96},{96,112},{112,128},... | collective-permute-start | bytes 18440 | tf_op jit(solution)/shard_map/ppermute | solution.py:19
  217.7 18.2 %collective-permute-start.13 = (f32[1,1,12,128]{3,2,1,0:T(8,128)S(1)}, f32[1,1,12,128]{3,2,1,0:T(8,128)S(1)}, u32[]{:S(2)}, u32[]{:S(2)}) collective-permute-start(f32[1,1,12,128]{3,2,1,0:T(8,128)S(1)} %bitcast.76), channel_id=1, source_target_pairs={{16,0},{32,16},{48,32},{64,48},{80,64},{96,80},{112,96},{128,112},... | collective-permute-start | bytes 18440 | tf_op jit(solution)/shard_map/ppermute | solution.py:22
  226.4 18.7 %collective-permute-start.22 = (f32[3,1,12,128]{3,2,1,0:T(8,128)S(1)}, f32[3,1,12,128]{3,2,1,0:T(8,128)S(1)}, u32[]{:S(2)}, u32[]{:S(2)}) collective-permute-start(f32[3,1,12,128]{3,2,1,0:T(8,128)S(1)} %pad_maximum_fusion.5), channel_id=1, source_target_pairs={{0,1},{1,2},{2,3},{3,4},{4,5},{5,6},{6,7},{7,8},{8,9},{9,10},{10,1... | collective-permute-start | bytes 55304 | tf_op jit(solution)/shard_map/ppermute | solution.py:19
  233.9 11.2 %collective-permute-start.23 = (f32[3,1,12,128]{3,2,1,0:T(8,128)S(1)}, f32[3,1,12,128]{3,2,1,0:T(8,128)S(1)}, u32[]{:S(2)}, u32[]{:S(2)}) collective-permute-start(f32[3,1,12,128]{3,2,1,0:T(8,128)S(1)} %pad_maximum_fusion.5), channel_id=1, source_target_pairs={{1,0},{2,1},{3,2},{4,3},{5,4},{6,5},{7,6},{8,7},{9,8},{10,9},{11,1... | collective-permute-start | bytes 55304 | tf_op jit(solution)/shard_map/ppermute | solution.py:22
  235.9 9.3 %collective-permute-start.14 = (f32[3,1,12,128]{3,2,1,0:T(8,128)S(1)}, f32[3,1,12,128]{3,2,1,0:T(8,128)S(1)}, u32[]{:S(2)}, u32[]{:S(2)}) collective-permute-start(f32[3,1,12,128]{3,2,1,0:T(8,128)S(1)} %pad_maximum_fusion.4), channel_id=1, source_target_pairs={{0,1},{1,2},{2,3},{3,4},{4,5},{5,6},{6,7},{7,8},{8,9},{9,10},{10,1... | collective-permute-start | bytes 55304 | tf_op jit(solution)/shard_map/ppermute | solution.py:19
  243.2 8.8 %collective-permute-start.15 = (f32[3,1,12,128]{3,2,1,0:T(8,128)S(1)}, f32[3,1,12,128]{3,2,1,0:T(8,128)S(1)}, u32[]{:S(2)}, u32[]{:S(2)}) collective-permute-start(f32[3,1,12,128]{3,2,1,0:T(8,128)S(1)} %pad_maximum_fusion.4), channel_id=1, source_target_pairs={{1,0},{2,1},{3,2},{4,3},{5,4},{6,5},{7,6},{8,7},{9,8},{10,9},{11,1... | collective-permute-start | bytes 55304 | tf_op jit(solution)/shard_map/ppermute | solution.py:22
  350.6 0.7 copy-start.3
  350.6 0.9 copy-start.4
where the time goes:
time: 356 us; the launch traced here: 351 us
  matrix products  107 us (30%)
  starting transfers between devices  105 us (29%)
  other arithmetic  62.9 us (18%)
  local copies, waits for them, and re-layouts  61 us (17%)
  waiting for transfers between devices  12.4 us (3%)
    dot_general x72, matrix products, contract(): lax.dot_general(left, right, (((left_dim,), (right_dim,)), ((), ())), pre...  107 us
    ppermute x12, starting transfers between devices, with_halo(): lax.ppermute(lax.slice_in_dim(block, block.shape[dim] - width, None, axis...  54.2 us
    ppermute x12, starting transfers between devices, with_halo(): lax.ppermute(lax.slice_in_dim(block, 0, width, axis=dim), axis, backward)  50.8 us
    and x24, other arithmetic, pair_table(): (jnp.abs(step_t) <= window_row[0]) & (jnp.abs(step_h) <= window_row[1])  31.3 us
    and x24, other arithmetic, pair_table(): return reach & (listed > 0) & inside  15.3 us
    slice x24, local copies, waits for them, and re-layouts, pair_table(): window_row[0]  14.4 us
    ppermute x12, waiting for transfers between devices, with_halo(): lax.ppermute(lax.slice_in_dim(block, 0, width, axis=dim), axis, backward)  12.4 us
    concatenate x6, other arithmetic, with_halo(): block = jnp.concatenate([low, block, high], axis=dim)  10.4 us
  transfers between devices with their start and end apart: 24, of which 2 were waited for; matrix products, arithmetic and copies ran while one was open for 38% of the time, Pallas kernels for 0%

commit v1 on v0

v1 whole, which is shorter than its diff:
```python
import functools
import math

import jax
import jax.numpy as jnp
from jax import lax
from jax.experimental import pallas as pl
from jax.experimental.pallas import tpu as pltpu
from jax.sharding import PartitionSpec as P

TILE = 32
NEG = -1e30
K, V, Q, G = 0, 1, 2, 3
MESH = pl.DeviceIdType.MESH


def dot_nt(a, b):
    return lax.dot_general(a, b, (((1,), (1,)), ((), ())), preferred_element_type=jnp.float32)


def dot_nn(a, b):
    return lax.dot_general(a, b, (((1,), (0,)), ((), ())), preferred_element_type=jnp.float32)


def dot_tn(a, b):
    return lax.dot_general(a, b, (((0,), (0,)), ((), ())), preferred_element_type=jnp.float32)


def fused_kernel(
    n, half, heads, tc, hc, slab, width,
    penalty, own,
    o_out, dq_out, dk_out, dv_out,
    rt, rh, rd, dk_acc, dv_acc, stats_col, stats, stats_in,
    tsend, trecv, hsend, hrecv, dsend, drecv, ssend, srecv,
):
    scale = 1.0 / math.sqrt(width)
    t = lax.axis_index("tm")
    h = lax.axis_index("height")
    rest = half - n
    t_near = (jnp.maximum(t - 1, 0), jnp.minimum(t + 1, tc - 1))
    h_near = (jnp.maximum(h - 1, 0), jnp.minimum(h + 1, hc - 1))
    has_t = (t > 0, t < tc - 1)
    has_h = (h > 0, h < hc - 1)

    barrier = pltpu.get_barrier_semaphore()
    for a in (-1, 0, 1):
        for b in (-1, 0, 1):
            if a == 0 and b == 0:
                continue
            ok = True
            if a != 0:
                ok = has_t[(a + 1) // 2]
            if b != 0:
                ok = jnp.logical_and(ok, has_h[(b + 1) // 2])

            @pl.when(ok)
            def _(a=a, b=b):
                pl.semaphore_signal(barrier, inc=1, device_id=(t + a, h + b), device_id_type=MESH)

    for d in (0, 1):
        @pl.when(jnp.logical_not(has_t[d]))
        def _(d=d):
            rt[d] = jnp.zeros(rt.shape[1:], rt.dtype)

        @pl.when(jnp.logical_not(has_h[d]))
        def _(d=d):
            rh[d] = jnp.zeros(rh.shape[1:], rh.dtype)

        if n:
            for e in (0, 1):
                @pl.when(jnp.logical_not(jnp.logical_and(has_h[d], has_t[e])))
                def _(d=d, e=e):
                    rd[d, e] = jnp.zeros(rd.shape[2:], rd.dtype)

    for a in range(3):
        for b in range(3):
            if a == 1 and b == 1:
                continue
            ok = True
            if a != 1:
                ok = has_t[a // 2]
            if b != 1:
                ok = jnp.logical_and(ok, has_h[b // 2])

            @pl.when(jnp.logical_not(ok))
            def _(a=a, b=b):
                stats_in[a, b] = jnp.zeros(stats_in.shape[2:], jnp.float32)

    count_t = has_t[0].astype(jnp.int32) + has_t[1].astype(jnp.int32)
    count_h = has_h[0].astype(jnp.int32) + has_h[1].astype(jnp.int32)
    pl.semaphore_wait(barrier, count_t + count_h + count_t * count_h)

    parts = []
    if n:
        parts.append((0, 0, n))
    if rest:
        parts.append((1, n, rest))

    def t_copy(array, part, d):
        index, first, size = part
        return pltpu.make_async_remote_copy(
            src_ref=own.at[array, pl.ds(first, size)],
            dst_ref=rt.at[1 - d, array, pl.ds(first, size)],
            send_sem=tsend.at[array, index, d],
            recv_sem=trecv.at[array, index, 1 - d],
            device_id=(t_near[d], h), device_id_type=MESH,
        )

    def h_copy(array, part, d):
        index, first, size = part
        source = 0 if index == 0 else half
        return pltpu.make_async_remote_copy(
            src_ref=own.at[array, pl.ds(source, size)],
            dst_ref=rh.at[1 - d, array, pl.ds(first, size)],
            send_sem=hsend.at[array, index, d],
            recv_sem=hrecv.at[array, index, 1 - d],
            device_id=(t, h_near[d]), device_id_type=MESH,
        )

    def d_copy(array, e, d):
        return pltpu.make_async_remote_copy(
            src_ref=rt.at[e, array, pl.ds(0, n)],
            dst_ref=rd.at[1 - d, e, array],
            send_sem=dsend.at[array, e, d],
            recv_sem=drecv.at[array, e, 1 - d],
            device_id=(t, h_near[d]), device_id_type=MESH,
        )

    for part in parts:
        for array in range(4):
            for d in (0, 1):
                @pl.when(has_t[d])
                def _(part=part, array=array, d=d):
                    t_copy(array, part, d).start()

                @pl.when(has_h[d])
                def _(part=part, array=array, d=d):
                    h_copy(array, part, d).start()

    if n:
        for array in range(4):
            for e in (0, 1):
                @pl.when(has_t[e])
                def _(array=array, e=e):
                    t_copy(array, parts[0], 1 - e).wait_recv()
                    for d in (0, 1):
                        @pl.when(has_h[d])
                        def _(d=d):
                            d_copy(array, e, d).start()

    for part in parts:
        for array in range(4):
            for e in (0, 1):
                if part[0] == 1:
                    @pl.when(has_t[e])
                    def _(part=part, array=array, e=e):
                        t_copy(array, part, 1 - e).wait_recv()

                @pl.when(has_h[e])
                def _(part=part, array=array, e=e):
                    h_copy(array, part, 1 - e).wait_recv()

    if n:
        for array in range(4):
            for d in (0, 1):
                for e in (0, 1):
                    @pl.when(jnp.logical_and(has_h[d], has_t[e]))
                    def _(array=array, d=d, e=e):
                        d_copy(array, e, 1 - d).wait_recv()

    def inside(dt, dr):
        ok = True
        if dt:
            ok = has_t[(dt + 1) // 2]
        if dr:
            ok = jnp.logical_and(ok, has_h[(dr + 1) // 2])
        return ok

    row_tile = lax.broadcasted_iota(jnp.int32, (slab, slab), 0) // TILE
    col_tile = lax.broadcasted_iota(jnp.int32, (slab, slab), 1) // TILE
    step = col_tile - row_tile

    def masked(scores, slot, dt, dr, sign):
        first = 9 * (sign * dt + 1) + 3 * (sign * dr + 1) + 1
        added = jnp.full((slab, slab), NEG, jnp.float32)
        for dw in (-1, 0, 1):
            value = penalty[slot, first + dw]
            if dt or dr:
                value = jnp.where(inside(dt, dr), value, NEG)
            added = jnp.where(step == sign * dw, value, added)
        return scores * scale + added

    def block(dt, dr, array, slot):
        if dr == 0:
            return rt[(dt + 1) // 2, array, slot]
        if dt == 0:
            return rh[(dr + 1) // 2, array, slot]
        return rd[(dr + 1) // 2, (dt + 1) // 2, array, slot]

    lane = lax.broadcasted_iota(jnp.int32, (slab, slab), 1)
    stats_col[...] = jnp.zeros((slab, slab), jnp.float32)

    def first_pass(slot, at, offsets):
        query = own[Q, slot]
        cot = own[G, slot]

        def get(array, dt, dr):
            if dt == 0 and dr == 0:
                return own[array, slot]
            return block(dt, dr, array, at)

        scores = []
        for dt, dr in offsets:
            scores.append(masked(dot_nt(query, get(K, dt, dr)), slot, dt, dr, 1))
        highest = scores[0]
        for part in scores[1:]:
            highest = jnp.maximum(highest, part)
        highest = jnp.max(highest, axis=1, keepdims=True)
        weights = [jnp.exp(part - highest) for part in scores]
        total = weights[0]
        for part in weights[1:]:
            total = total + part
        total = jnp.sum(total, axis=1, keepdims=True)
        inverse = 1.0 / total
        out = jnp.zeros((slab, width), jnp.float32)
        probs = []
        for (dt, dr), part in zip(offsets, weights):
            prob = part * inverse
            probs.append(prob)
            out = out + dot_nn(prob.astype(jnp.bfloat16), get(V, dt, dr))
        out = out.astype(jnp.bfloat16)
        o_out[slot] = out
        delta = jnp.sum(cot.astype(jnp.float32) * out.astype(jnp.float32), axis=1, keepdims=True)
        grad = jnp.zeros((slab, width), jnp.float32)
        for (dt, dr), prob in zip(offsets, probs):
            slope = dot_nt(cot, get(V, dt, dr))
            slope = (prob * (slope - delta)).astype(jnp.bfloat16)
            grad = grad + dot_nn(slope, get(K, dt, dr))
            if dt == 0 and dr == 0:
                dk_acc[slot] = dot_tn(slope, query)
                dv_acc[slot] = dot_tn(prob.astype(jnp.bfloat16), cot)
        dq_out[slot] = (grad * scale).astype(jnp.bfloat16)
        log_sum = highest + jnp.log(total)
        held = jnp.where(lane == slot, log_sum, stats_col[...])
        stats_col[...] = jnp.where(lane == slot + 16, delta, held)

    centre = [(0, 0)]
    t_only = [(-1, 0), (1, 0)]
    h_only = [(0, -1), (0, 1)]
    corners = [(-1, -1), (-1, 1), (1, -1), (1, 1)]

    def loop(count, body):
        if count:
            lax.fori_loop(0, count, lambda i, c: (body(i), c)[1], 0)

    loop(n, lambda i: first_pass(i, i, centre + t_only + h_only + corners))
    loop(rest, lambda i: first_pass(n + i, n + i, centre + t_only))
    loop(rest, lambda i: first_pass(half + i, n + i, centre + h_only))
    loop(n, lambda i: first_pass(half + rest + i, 0, centre))

    stats[...] = jnp.transpose(stats_col[...])[: stats.shape[0]]

    def s_copy(a, b):
        return pltpu.make_async_remote_copy(
            src_ref=stats,
            dst_ref=stats_in.at[1 - a, 1 - b],
            send_sem=ssend.at[a + 1, b + 1],
            recv_sem=srecv.at[1 - a, 1 - b],
            device_id=(t_near[(a + 1) // 2] if a else t, h_near[(b + 1) // 2] if b else h),
            device_id_type=MESH,
        )

    near = t_only + h_only + corners
    for a, b in near:
        @pl.when(inside(a, b))
        def _(a=a, b=b):
            s_copy(a, b).start()
    for a, b in near:
        @pl.when(inside(a, b))
        def _(a=a, b=b):
            s_copy(-a, -b).wait_recv()

    def second_pass(slot, at, offsets):
        key = own[K, slot]
        val = own[V, slot]
        dk = dk_acc[slot]
        dv = dv_acc[slot]
        for dt, dr in offsets:
            query = block(dt, dr, Q, at)
            cot = block(dt, dr, G, at)
            log_sum = stats_in[dt + 1, dr + 1, pl.ds(slot, 1), :]
            delta = stats_in[dt + 1, dr + 1, pl.ds(slot + 16, 1), :]
            part = masked(dot_nt(key, query), slot, dt, dr, -1)
            prob = jnp.exp(part - log_sum)
            dv = dv + dot_nn(prob.astype(jnp.bfloat16), cot)
            slope = dot_nt(val, cot)
            slope = (prob * (slope - delta)).astype(jnp.bfloat16)
            dk = dk + dot_nn(slope, query)
        dk_out[slot] = (dk * scale).astype(jnp.bfloat16)
        dv_out[slot] = dv.astype(jnp.bfloat16)

    loop(n, lambda i: second_pass(i, i, near))
    loop(rest, lambda i: second_pass(n + i, n + i, t_only))
    loop(rest, lambda i: second_pass(half + i, n + i, h_only))
    loop(n, lambda i: second_pass(half + rest + i, 0, []))

    for part in parts:
        for array in range(4):
            for d in (0, 1):
                @pl.when(has_t[d])
                def _(part=part, array=array, d=d):
                    t_copy(array, part, d).wait_send()

                @pl.when(has_h[d])
                def _(part=part, array=array, d=d):
                    h_copy(array, part, d).wait_send()
    if n:
        for array in range(4):
            for e in (0, 1):
                for d in (0, 1):
                    @pl.when(jnp.logical_and(has_h[d], has_t[e]))
                    def _(array=array, d=d, e=e):
                        d_copy(array, e, d).wait_send()
    for a, b in near:
        @pl.when(inside(a, b))
        def _(a=a, b=b):
            s_copy(a, b).wait_send()


def pack_kernel(
    heads, width, window, mask, k_in, v_in, q_in, g_in, packed, penalty, slots
):
    half = heads // 2
    time = [window[i, 0] for i in range(heads)]
    height = [window[i, 1] for i in range(heads)]
    both = [x * y for x, y in zip(time, height)]
    total = functools.reduce(lambda x, y: x + y, both)
    seen = [0, total, half, 2 * half - total]
    for i in range(heads):
        kind = [both[i], time[i] - both[i], height[i] - both[i], 1 - time[i] - height[i] + both[i]]
        slot = sum(k * c for k, c in zip(kind, seen))
        seen = [c + k for k, c in zip(kind, seen)]
        slots[i] = slot
        for number, ref in ((K, k_in), (V, v_in), (Q, q_in), (G, g_in)):
            packed[number, slot] = ref[:, i * width : (i + 1) * width]
        for offset in range(27):
            allowed = mask[i, offset] == 1
            for axis, moved in enumerate((offset // 9 != 1, offset // 3 % 3 != 1, offset % 3 != 1)):
                if moved:
                    allowed = jnp.logical_and(allowed, window[i, axis] == 1)
            penalty[slot, offset] = jnp.where(allowed, 0.0, NEG).astype(jnp.float32)


def spread_kernel(heads, width, slots, o_in, dq_in, dk_in, dv_in, o_out, dq_out, dk_out, dv_out):
    for source, target in ((o_in, o_out), (dq_in, dq_out), (dk_in, dk_out), (dv_in, dv_out)):
        for i in range(heads):
            target[:, i * width : (i + 1) * width] = source[slots[i]]


def on_device(tc, hc, query_vecs, key_vecs, value_vecs, grad_output, tile_window, neighbour_mask):
    slab, features = query_vecs.shape[2:]
    heads = tile_window.shape[0]
    half = heads // 2
    width = features // heads
    both = jnp.sum(tile_window[:, 0] * tile_window[:, 1])
    vmem = pl.BlockSpec(memory_space=pltpu.VMEM)
    smem = pl.BlockSpec(memory_space=pltpu.SMEM)
    packed = jax.ShapeDtypeStruct((heads, slab, width), jnp.bfloat16)
    dma = pltpu.SemaphoreType.DMA

    def branch(n):
        def run(penalty, own):
            return pl.pallas_call(
                functools.partial(fused_kernel, n, half, heads, tc, hc, slab, width),
                out_shape=(packed,) * 4,
                in_specs=[smem, vmem],
                out_specs=(vmem,) * 4,
                scratch_shapes=[
                    pltpu.VMEM((2, 4, half, slab, width), jnp.bfloat16),
                    pltpu.VMEM((2, 4, half, slab, width), jnp.bfloat16),
                    pltpu.VMEM((2, 2, 4, max(n, 1), slab, width), jnp.bfloat16),
                    pltpu.VMEM((heads, slab, width), jnp.float32),
                    pltpu.VMEM((heads, slab, width), jnp.float32),
                    pltpu.VMEM((slab, slab), jnp.float32),
                    pltpu.VMEM((32, slab), jnp.float32),
                    pltpu.VMEM((3, 3, 32, slab), jnp.float32),
                    dma((4, 2, 2)), dma((4, 2, 2)),
                    dma((4, 2, 2)), dma((4, 2, 2)),
                    dma((4, 2, 2)), dma((4, 2, 2)),
                    dma((3, 3)), dma((3, 3)),
                ],
                compiler_params=pltpu.CompilerParams(
                    collective_id=n, has_side_effects=True, vmem_limit_bytes=60 * 1024 * 1024
                ),
                name=f"tiles_{n}",
            )(penalty, own)
        return run

    arrays = [x.reshape(slab, features) for x in (key_vecs, value_vecs, query_vecs, grad_output)]
    own, penalty, slots = pl.pallas_call(
        functools.partial(pack_kernel, heads, width),
        out_shape=(
            jax.ShapeDtypeStruct((4, heads, slab, width), jnp.bfloat16),
            jax.ShapeDtypeStruct((heads, 27), jnp.float32),
            jax.ShapeDtypeStruct((heads,), jnp.int32),
        ),
        in_specs=[smem, smem] + [vmem] * 4,
        out_specs=(vmem, smem, smem),
        name="pack",
    )(tile_window, neighbour_mask, *arrays)
    results = lax.switch(both, [branch(n) for n in range(half + 1)], penalty, own)
    flat = jax.ShapeDtypeStruct((slab, features), jnp.bfloat16)
    outs = pl.pallas_call(
        functools.partial(spread_kernel, heads, width),
        out_shape=(flat,) * 4,
        in_specs=[smem] + [vmem] * 4,
        out_specs=(vmem,) * 4,
        name="spread",
    )(slots, *results)
    return tuple(x.reshape(1, 1, slab, features) for x in outs)


def solution(mesh):
    split = P("tm", "height", None, None)
    return jax.shard_map(
        functools.partial(on_device, mesh.shape["tm"], mesh.shape["height"]),
        mesh=mesh,
        in_specs=(split,) * 4 + (P(), P()),
        out_specs=(split,) * 4,
        check_vma=False,
    )
```

time: 356 us -> 77.3 us (0.22)
  the two profiles are of different devices: /device:TPU:27 before, /device:TPU:25 now
where the time goes in v1:
time: 77.3 us; the launch traced here: 77.1 us
  Pallas kernels  72.4 us (94%)
  other arithmetic  1.4 us (2%)
  local copies, waits for them, and re-layouts  1.36 us (2%)
  between operations  1.3 us (2%)
    pallas_call x1, Pallas kernels, run(): pl.pallas_call(functools.partial(fused_kernel, n, half, heads, tc, hc, sl...  67.1 us
    pallas_call x1, Pallas kernels, on_device(): pl.pallas_call(functools.partial(pack_kernel, heads, width), out_shape=(j...  3.28 us
    pallas_call x1, Pallas kernels, on_device(): pl.pallas_call(functools.partial(spread_kernel, heads, width), out_shape=...  2.08 us

profile of v1, /device:TPU:25, one launch (start us, length us, event | category | flops | bytes accessed | tf_op | source)
XLA Modules:
  0.0 77.1 jit_solution(14448484574039603206)
XLA Ops:
  0.6 1.4 %multiply_reduce_fusion = s32[]{:T(128)} fusion(s32[12,3]{0,1:T(4,128)} %param.17), kind=kLoop, calls=%fused_computation | loop fusion | flops 23 | bytes 100 | tf_op jit(solution)/shard_map/reduce_sum | solution.py:365
  2.7 1.4 %copy.10.window = s32[12,3]{1,0:T(8,128)} copy(s32[12,3]{0,1:T(4,128)} %param.17) | data formatting | bytes 288 | tf_op args[4]
  4.0 3.3 %pack.1 = (bf16[4,12,128,128]{3,2,1,0:T(8,128)(2,1)S(1)}, f32[12,27]{1,0:T(8,128)S(1)}, s32[12]{0:T(128)}) custom-call(s32[12,3]{1,0:T(8,128)} %copy.10.window, s32[12,27]{1,0:T(8,128)} %mask.1, bf16[128,1536]{1,0:T(8,128)(2,1)} %bitcast.8, bf16[128,1536]{1,0:T(8,128)(2,1)} %bitcast.9, bf16[128,1536]{1,0:T(8,128)(2,1)} %bitcast.10, bf16[128,1536]{1,0:T(8,128)(2,1)} %bitcast.11), custom_call_target="tpu_custom_call" | custom-call | tf_op jit(solution)/shard_map/pack/pallas_call | solution.py:400
  7.3 67.6 %conditional.1 = ((bf16[12,128,128]{2,1,0:T(8,128)(2,1)S(1)}, bf16[12,128,128]{2,1,0:T(8,128)(2,1)S(1)}, bf16[12,128,128]{2,1,0:T(8,128)(2,1)S(1)}, bf16[12,128,128]{2,1,0:T(8,128)(2,1)S(1)})) conditional(s32[]{:T(128)} %clamp.3, (f32[12,27]{1,0:T(8,128)S(1)}, bf16[4,12,128,128]{3,2,1,0:T(8,128)(2,1)S(1)}) %tuple.29, ...), branch_computations={%region_1.0_spmd, %region_2.0_spmd, %region_3.0_spmd, %region_4.0_... | conditional | bytes 8 | solution.py:411
  7.4 67.1 %tiles_2.1 = (bf16[12,128,128]{2,1,0:T(8,128)(2,1)S(1)}, bf16[12,128,128]{2,1,0:T(8,128)(2,1)S(1)}, bf16[12,128,128]{2,1,0:T(8,128)(2,1)S(1)}, bf16[12,128,128]{2,1,0:T(8,128)(2,1)S(1)}) custom-call(f32[12,27]{1,0:T(8,128)S(1)} %get-tuple-element.32.penalty, bf16[4,12,128,128]{3,2,1,0:T(8,128)(2,1)S(1)} %get-tuple-element.33.own), custom_call_target="tpu_custom_call" | custom-call | tf_op jit(solution)/shard_map/cond/branch_2_fun/tiles_2/pallas_call | solution.py:373
  75.0 2.1 %spread.1 = (bf16[128,1536]{1,0:T(8,128)(2,1)}, bf16[128,1536]{1,0:T(8,128)(2,1)}, bf16[128,1536]{1,0:T(8,128)(2,1)}, bf16[128,1536]{1,0:T(8,128)(2,1)}) custom-call(s32[12]{0:T(128)} %get-tuple-element.57.slots, bf16[12,128,128]{2,1,0:T(8,128)(2,1)S(1)} %get-tuple-element.60.o_in, bf16[12,128,128]{2,1,0:T(8,128)(2,1)S(1)} %get-tuple-element.61.dq_in, ...), custom_call_target="tpu_custom_call" | custom-call | tf_op jit(solution)/shard_map/spread/pallas_call | solution.py:413

commit v2 on v1

v2 whole, which is shorter than its diff:
```python
import functools
import math

import jax
import jax.numpy as jnp
from jax import lax
from jax.experimental import pallas as pl
from jax.experimental.pallas import tpu as pltpu
from jax.sharding import PartitionSpec as P

TILE = 32
NEG = -1e30
K, V, Q, G = 0, 1, 2, 3
MESH = pl.DeviceIdType.MESH
LOG2E = 1.0 / math.log(2.0)


def dot_nt(a, b):
    return lax.dot_general(a, b, (((1,), (1,)), ((), ())), preferred_element_type=jnp.float32)


def dot_nn(a, b):
    return lax.dot_general(a, b, (((1,), (0,)), ((), ())), preferred_element_type=jnp.float32)


def fused_kernel(
    n, rest, alone, tc, hc, slab, width,
    penalty, own,
    o_out, dq_out, dk_out, dv_out,
    xb, xt, xh, stats_col, stats, stats_in,
    lsend, esend, zsend, tsend, trecv, hsend, hrecv, dsend, drecv, ssend, srecv,
):
    scale = 1.0 / math.sqrt(width)
    half = n + rest
    t = lax.axis_index("tm")
    h = lax.axis_index("height")
    t_near = (jnp.maximum(t - 1, 0), jnp.minimum(t + 1, tc - 1))
    h_near = (jnp.maximum(h - 1, 0), jnp.minimum(h + 1, hc - 1))
    has_t = (t > 0, t < tc - 1)
    has_h = (h > 0, h < hc - 1)
    centre = [(0, 0)]
    t_line = [(-1, 0), (0, 0), (1, 0)]
    h_line = [(0, -1), (0, 0), (0, 1)]
    square = [(dt, dr) for dt in (-1, 0, 1) for dr in (-1, 0, 1)]
    around = [x for x in square if x != (0, 0)]

    def inside(dt, dr):
        ok = True
        if dt:
            ok = has_t[(dt + 1) // 2]
        if dr:
            ok = jnp.logical_and(ok, has_h[(dr + 1) // 2])
        return ok

    def when(ok, body):
        if ok is True:
            body()
        else:
            pl.when(ok)(body)

    cross = {-1: h == hc // 2, 1: h == hc // 2 - 1}
    outer = jnp.logical_or(t == 0, t == tc - 1)
    inner = {-1: t == 1, 1: t == tc - 2}
    near_end = jnp.logical_or(inner[-1], inner[1])

    def both_of(a, b):
        return b if a is True else jnp.logical_and(a, b)

    barrier = pltpu.get_barrier_semaphore()
    for dt, dr in around:
        def greet(dt=dt, dr=dr):
            pl.semaphore_signal(barrier, inc=1, device_id=(t + dt, h + dr), device_id_type=MESH)
        when(inside(dt, dr), greet)

    local = []
    if n:
        local.append(pltpu.make_async_copy(own.at[:, pl.ds(0, n)], xb.at[:, :, 4], lsend.at[0]))
    if rest:
        local.append(pltpu.make_async_copy(own.at[:, pl.ds(n, rest)], xt.at[:, :, 1], lsend.at[1]))
        local.append(pltpu.make_async_copy(own.at[:, pl.ds(half, rest)], xh.at[:, :, 1], lsend.at[2]))
    for copy in local:
        copy.start()

    fill = []
    for dt, dr in around:
        def add(source, target, number, dt=dt, dr=dr):
            copy = pltpu.make_async_copy(source, target, esend.at[number])
            fill.append((jnp.logical_not(inside(dt, dr)), copy))
        if n:
            add(own.at[:, pl.ds(0, n)], xb.at[:, :, 3 * (dt + 1) + dr + 1], 3 * (dt + 1) + dr + 1)
        if rest and dr == 0:
            add(own.at[:, pl.ds(n, rest)], xt.at[:, :, dt + 1], 10 + dt)
        if rest and dt == 0:
            add(own.at[:, pl.ds(half, rest)], xh.at[:, :, dr + 1], 13 + dr)

        def clear(dt=dt, dr=dr):
            stats_in[dt + 1, dr + 1] = jnp.zeros(stats_in.shape[2:], jnp.float32)
        when(jnp.logical_not(inside(dt, dr)), clear)
    for ok, copy in fill:
        when(ok, copy.start)
    stats_col[...] = jnp.zeros((slab, slab), jnp.float32)

    count_t = has_t[0].astype(jnp.int32) + has_t[1].astype(jnp.int32)
    count_h = has_h[0].astype(jnp.int32) + has_h[1].astype(jnp.int32)
    pl.semaphore_wait(barrier, count_t + count_h + count_t * count_h)

    def t_copy(array, part, d):
        if part == 0:
            source, target = own.at[array, pl.ds(0, n)], xb.at[array, :, 3 * (1 - d) + 1]
        else:
            source, target = own.at[array, pl.ds(n, rest)], xt.at[array, :, 1 - d]
        return pltpu.make_async_remote_copy(
            src_ref=source, dst_ref=target,
            send_sem=tsend.at[array, part, d + 1], recv_sem=trecv.at[array, part, 1 - d],
            device_id=(t_near[(d + 1) // 2], h), device_id_type=MESH,
        )

    def h_copy(array, part, d):
        if part == 0:
            source, target = own.at[array, pl.ds(0, n)], xb.at[array, :, 3 + 1 - d]
        else:
            source, target = own.at[array, pl.ds(half, rest)], xh.at[array, :, 1 - d]
        return pltpu.make_async_remote_copy(
            src_ref=source, dst_ref=target,
            send_sem=hsend.at[array, part, d + 1], recv_sem=hrecv.at[array, part, 1 - d],
            device_id=(t, h_near[(d + 1) // 2]), device_id_type=MESH,
        )

    def d_copy(array, e, d):
        return pltpu.make_async_remote_copy(
            src_ref=xb.at[array, :, 3 * (e + 1) + 1], dst_ref=xb.at[array, :, 3 * (e + 1) + 1 - d],
            send_sem=dsend.at[array, e + 1, d + 1], recv_sem=drecv.at[array, e + 1, 1 - d],
            device_id=(t, h_near[(d + 1) // 2]), device_id_type=MESH,
        )

    def z_copy(array, f, d):
        return pltpu.make_async_remote_copy(
            src_ref=xb.at[array, :, 4 + d], dst_ref=xb.at[array, :, 3 * (1 - f) + 1 + d],
            send_sem=zsend.at[array], recv_sem=drecv.at[array, 1 - f, d + 1],
            device_id=(t_near[(f + 1) // 2], h), device_id_type=MESH,
        )

    def s_copy(group, dt, dr):
        return pltpu.make_async_remote_copy(
            src_ref=stats.at[group], dst_ref=stats_in.at[1 - dt, 1 - dr, group],
            send_sem=ssend.at[group, dt + 1, dr + 1], recv_sem=srecv.at[group, 1 - dt, 1 - dr],
            device_id=(t_near[(dt + 1) // 2] if dt else t, h_near[(dr + 1) // 2] if dr else h),
            device_id_type=MESH,
        )

    both, lone = n > 0, rest > 0

    def t_start(array, part):
        for d in (-1, 1):
            when(inside(d, 0), lambda d=d: t_copy(array, part, d).start())

    def h_start(array, part, ok=True):
        for d in (-1, 1):
            when(both_of(ok, inside(0, d)), lambda d=d: h_copy(array, part, d).start())

    def t_wait(array, part):
        for e in (-1, 1):
            when(inside(e, 0), lambda e=e: t_copy(array, part, -e).wait_recv())

    def h_wait(array, part):
        for e in (-1, 1):
            ok = inside(0, e)
            if part == 0:
                ok = both_of(ok, jnp.logical_not(jnp.logical_and(near_end, cross[e])))
            when(ok, lambda e=e: h_copy(array, part, -e).wait_recv())

    def z_relay(array):
        for d in (-1, 1):
            for f in (-1, 1):
                def forward(d=d, f=f):
                    h_copy(array, 0, -d).wait_recv()
                    z_copy(array, f, d).start()
                when(jnp.logical_and(inner[f], cross[d]), forward)

    def relay(array):
        for e in (-1, 1):
            def forward(e=e):
                t_copy(array, 0, -e).wait_recv()
                for d in (-1, 1):
                    ok = jnp.logical_and(inside(0, d), jnp.logical_not(jnp.logical_and(outer, cross[d])))
                    when(ok, lambda d=d: d_copy(array, e, d).start())
            when(inside(e, 0), forward)

    def d_wait(array):
        for e in (-1, 1):
            for d in (-1, 1):
                when(inside(e, d), lambda e=e, d=d: d_copy(array, e, -d).wait_recv())

    def s_start(group, steps):
        for dt, dr in steps:
            when(inside(dt, dr), lambda dt=dt, dr=dr: s_copy(group, dt, dr).start())

    def s_wait(group, steps):
        for dt, dr in steps:
            when(inside(dt, dr), lambda dt=dt, dr=dr: s_copy(group, -dt, -dr).wait_recv())

    row_tile = lax.broadcasted_iota(jnp.int32, (slab, slab), 0) // TILE
    col_tile = lax.broadcasted_iota(jnp.int32, (slab, slab), 1) // TILE
    step = col_tile - row_tile
    lane = lax.broadcasted_iota(jnp.int32, (slab, slab), 1)

    def added(slot, dt, dr, sign, minus=None):
        first = 9 * (sign * dt + 1) + 3 * (sign * dr + 1) + 1
        total = jnp.full((slab, slab), NEG, jnp.float32)
        for dw in (-1, 0, 1):
            value = penalty[slot, first + dw]
            if dt or dr:
                value = jnp.where(inside(dt, dr), value, NEG)
            if minus is not None:
                value = value - minus
            total = jnp.where(step == sign * dw, value, total)
        return total

    def first_pass(slot, blocks, get):
        query, cot, keys, values = own[Q, slot], own[G, slot], get(K), get(V)
        scores = dot_nt(query, keys) * (scale * LOG2E)
        scores = scores + jnp.concatenate([added(slot, dt, dr, 1) for dt, dr in blocks], axis=1)
        highest = jnp.max(scores, axis=1, keepdims=True)
        weights = jnp.exp2(scores - highest)
        total = jnp.sum(weights, axis=1, keepdims=True)
        inverse = 1.0 / total
        out = (dot_nn(weights.astype(jnp.bfloat16), values) * inverse).astype(jnp.bfloat16)
        o_out[slot] = out
        delta = jnp.sum(cot.astype(jnp.float32) * out.astype(jnp.float32), axis=1, keepdims=True)
        slope = (weights * (dot_nt(cot, values) - delta)).astype(jnp.bfloat16)
        dq_out[slot] = (dot_nn(slope, keys) * (inverse * scale)).astype(jnp.bfloat16)
        log_sum = highest + jnp.log2(total)
        held = jnp.where(lane == slot, log_sum, stats_col[...])
        stats_col[...] = jnp.where(lane == slot + 16, delta, held)

    def second_pass(group, slot, blocks, get):
        key, value, queries, cots = own[K, slot], own[V, slot], get(Q), get(G)
        scores = dot_nt(key, queries) * (scale * LOG2E)
        shifts, deltas = [], []
        for dt, dr in blocks:
            source = stats_in.at[dt + 1, dr + 1, group] if dt or dr else stats.at[group]
            shifts.append(added(slot, dt, dr, -1, source[pl.ds(slot, 1), :]))
            deltas.append(source[pl.ds(slot + 16, 1), :])
        probs = jnp.exp2(scores + jnp.concatenate(shifts, axis=1))
        dv_out[slot] = dot_nn(probs.astype(jnp.bfloat16), cots).astype(jnp.bfloat16)
        slope = dot_nt(value, cots) - jnp.concatenate(deltas, axis=1)
        slope = (probs * slope).astype(jnp.bfloat16)
        dk_out[slot] = (dot_nn(slope, queries) * scale).astype(jnp.bfloat16)

    def loop(count, body, pair=1):
        group = count if n == rest else pair if count % 2 == 0 else 1
        if count == group:
            for i in range(count):
                body(i)
        else:
            def several(i, carry):
                for j in range(group):
                    body(group * i + j)
                return carry
            lax.fori_loop(0, count // group, several, 0)

    def slabs(ref, i):
        return lambda array: ref[array, i].reshape(-1, width)

    def first_both():
        loop(n, lambda i: first_pass(i, square, slabs(xb, i)), 2)

    def first_time():
        loop(rest, lambda i: first_pass(n + i, t_line, slabs(xt, i)))

    def first_height():
        loop(rest, lambda i: first_pass(half + i, h_line, slabs(xh, i)))

    def first_alone():
        loop(alone, lambda i: first_pass(half + rest + i, centre, lambda array: own[array, half + rest + i]))

    def second_both():
        loop(n, lambda i: second_pass(0, i, square, slabs(xb, i)), 2)

    def second_time():
        loop(rest, lambda i: second_pass(1, n + i, t_line, slabs(xt, i)))

    def second_height():
        loop(rest, lambda i: second_pass(0, half + i, h_line, slabs(xh, i)))

    def second_alone():
        loop(alone, lambda i: second_pass(0, half + rest + i, centre, lambda array: own[array, half + rest + i]))

    def take_stats(group):
        stats[group] = jnp.transpose(stats_col[...])[: stats.shape[1]]

    if both:
        for array in range(4):
            t_start(array, 0)
            if array < 2:
                h_start(array, 0)
    if lone:
        for array in (K, V):
            t_start(array, 1)
            h_start(array, 1)
    for copy in local:
        copy.wait()
    for ok, copy in fill:
        when(ok, copy.wait)
    first_alone()
    if both:
        relay(K)
        relay(V)
        h_start(Q, 0)
        h_start(G, 0)
        z_relay(K)
        z_relay(V)
    if lone:
        h_wait(K, 1)
        h_wait(V, 1)
        first_height()
    slow = jnp.logical_and(outer, jnp.logical_or(cross[-1], cross[1]))
    if both:
        relay(Q)
        relay(G)
        z_relay(Q)
        z_relay(G)
    if lone:
        for array in (Q, G):
            h_start(array, 1, slow)
    if both:
        for array in (K, V):
            h_wait(array, 0)
            d_wait(array)
        first_both()
    take_stats(0)
    second_alone()
    s_start(0, around)
    if lone:
        for array in (Q, G):
            t_start(array, 1)
            h_start(array, 1, jnp.logical_not(slow))
        t_wait(K, 1)
        t_wait(V, 1)
        first_time()
        take_stats(1)
    s_wait(0, around)
    if lone:
        s_start(1, [(-1, 0), (1, 0)])
    if both:
        for array in (Q, G):
            h_wait(array, 0)
            d_wait(array)
        second_both()
    if lone:
        h_wait(Q, 1)
        h_wait(G, 1)
        second_height()
        t_wait(Q, 1)
        t_wait(G, 1)
        s_wait(1, [(-1, 0), (1, 0)])
        second_time()

    for array in range(4):
        for part in ([0] if both else []) + ([1] if lone else []):
            for d in (-1, 1):
                when(inside(d, 0), lambda array=array, part=part, d=d: t_copy(array, part, d).wait_send())
                when(inside(0, d), lambda array=array, part=part, d=d: h_copy(array, part, d).wait_send())
        if both:
            for e in (-1, 1):
                for d in (-1, 1):
                    ok = jnp.logical_and(inside(e, d), jnp.logical_not(jnp.logical_and(outer, cross[d])))
                    when(ok, lambda array=array, e=e, d=d: d_copy(array, e, d).wait_send())
            for d in (-1, 1):
                for f in (-1, 1):
                    when(jnp.logical_and(inner[f], cross[d]), z_copy(array, f, d).wait_send)
    for dt, dr in around:
        when(inside(dt, dr), lambda dt=dt, dr=dr: s_copy(0, dt, dr).wait_send())
    if lone:
        for d in (-1, 1):
            when(inside(d, 0), lambda d=d: s_copy(1, d, 0).wait_send())


def pack_kernel(
    heads, width, window, mask, k_in, v_in, q_in, g_in, packed, penalty, slots, kind_out
):
    half = heads // 2
    time = [window[0, i] for i in range(heads)]
    height = [window[1, i] for i in range(heads)]
    total = functools.reduce(lambda x, y: x + y, [x * y for x, y in zip(time, height)])
    few, many = total < 2, total > half - 2
    nb = jnp.where(few, 2, jnp.where(many, half, total))
    rest = jnp.where(few, half - 1, jnp.where(many, 1, half - total))
    alone = jnp.where(few, 0, jnp.where(many, half - 2, total))
    lone = half - total
    over = jnp.maximum(lone - rest, 0)
    spare_b = nb - total - 2 * over
    spare_t = jnp.maximum(rest - lone, 0)
    kind_out[0] = jnp.clip(total, 1, half - 1) - 1
    place = lax.broadcasted_iota(jnp.int32, (1, 27), 1)
    moved = (place // 9 != 1, place // 3 % 3 != 1, place % 3 != 1)
    seen = [0, 0, 0, 0]
    for i in range(heads):
        both = time[i] * height[i]
        kinds = [both, time[i] - both, height[i] - both, 1 - time[i] - height[i] + both]
        c = seen
        j = c[3] - alone
        slot = jnp.where(
            both == 1,
            c[0],
            jnp.where(
                time[i] == 1,
                jnp.where(c[1] < rest, nb + c[1], total + c[1] - rest),
                jnp.where(
                    height[i] == 1,
                    jnp.where(c[2] < rest, nb + rest + c[2], total + over + c[2] - rest),
                    jnp.where(
                        j < 0,
                        nb + 2 * rest + c[3],
                        jnp.where(
                            j < spare_b,
                            total + 2 * over + j,
                            jnp.where(j - spare_b < spare_t, nb + lone + j - spare_b, nb + rest + lone + j - spare_b - spare_t),
                        ),
                    ),
                ),
            ),
        )
        seen = [x + k for x, k in zip(c, kinds)]
        slots[i] = slot
        for number, ref in ((K, k_in), (V, v_in), (Q, q_in), (G, g_in)):
            packed[number, slot] = ref[:, i * width : (i + 1) * width]
        row = jnp.where(mask[i : i + 1, :] == 1, 0.0, NEG)
        for axis in range(3):
            row = jnp.where(moved[axis], row + jnp.where(window[axis, i] == 1, 0.0, NEG), row)
        penalty[pl.ds(slot, 1), :] = row


def class_sizes(half):
    return [(2, half - 1, 0)] + [(n, half - n, n) for n in range(2, half - 1)] + [(half, 1, half - 2)]


def spread_kernel(heads, width, slots, o_in, dq_in, dk_in, dv_in, o_out, dq_out, dk_out, dv_out):
    for source, target in ((o_in, o_out), (dq_in, dq_out), (dk_in, dk_out), (dv_in, dv_out)):
        for i in range(heads):
            target[:, i * width : (i + 1) * width] = source[slots[i]]


def on_device(tc, hc, query_vecs, key_vecs, value_vecs, grad_output, tile_window, neighbour_mask):
    slab, features = query_vecs.shape[2:]
    heads = tile_window.shape[0]
    half = heads // 2
    width = features // heads
    vmem = pl.BlockSpec(memory_space=pltpu.VMEM)
    smem = pl.BlockSpec(memory_space=pltpu.SMEM)
    packed = jax.ShapeDtypeStruct((heads, slab, width), jnp.bfloat16)
    dma = pltpu.SemaphoreType.DMA

    def branch(number, sizes):
        n, rest, alone = sizes

        def run(penalty, own):
            return pl.pallas_call(
                functools.partial(fused_kernel, n, rest, alone, tc, hc, slab, width),
                out_shape=(packed,) * 4,
                in_specs=[smem, vmem],
                out_specs=(vmem,) * 4,
                scratch_shapes=[
                    pltpu.VMEM((4, n, 9, slab, width), jnp.bfloat16),
                    pltpu.VMEM((4, rest, 3, slab, width), jnp.bfloat16),
                    pltpu.VMEM((4, rest, 3, slab, width), jnp.bfloat16),
                    pltpu.VMEM((slab, slab), jnp.float32),
                    pltpu.VMEM((2, 32, slab), jnp.float32),
                    pltpu.VMEM((3, 3, 2, 32, slab), jnp.float32),
                    dma((3,)), dma((15,)), dma((4,)),
                    dma((4, 2, 3)), dma((4, 2, 3)),
                    dma((4, 2, 3)), dma((4, 2, 3)),
                    dma((4, 3, 3)), dma((4, 3, 3)),
                    dma((2, 3, 3)), dma((2, 3, 3)),
                ],
                compiler_params=pltpu.CompilerParams(
                    collective_id=number, has_side_effects=True, vmem_limit_bytes=60 * 1024 * 1024
                ),
                name=f"tiles_{n}",
            )(penalty, own)
        return run

    arrays = [x.reshape(slab, features) for x in (key_vecs, value_vecs, query_vecs, grad_output)]
    own, penalty, slots, joint = pl.pallas_call(
        functools.partial(pack_kernel, heads, width),
        out_shape=(
            jax.ShapeDtypeStruct((4, heads, slab, width), jnp.bfloat16),
            jax.ShapeDtypeStruct((heads, 27), jnp.float32),
            jax.ShapeDtypeStruct((heads,), jnp.int32),
            jax.ShapeDtypeStruct((1,), jnp.int32),
        ),
        in_specs=[smem, vmem] + [vmem] * 4,
        out_specs=(vmem, vmem, smem, smem),
        name="pack",
    )(tile_window.T, neighbour_mask, *arrays)
    results = lax.switch(joint[0], [branch(i, x) for i, x in enumerate(class_sizes(half))], penalty, own)
    flat = jax.ShapeDtypeStruct((slab, features), jnp.bfloat16)
    outs = pl.pallas_call(
        functools.partial(spread_kernel, heads, width),
        out_shape=(flat,) * 4,
        in_specs=[smem] + [vmem] * 4,
        out_specs=(vmem,) * 4,
        name="spread",
    )(slots, *results)
    return tuple(x.reshape(1, 1, slab, features) for x in outs)


def solution(mesh):
    split = P("tm", "height", None, None)
    return jax.shard_map(
        functools.partial(on_device, mesh.shape["tm"], mesh.shape["height"]),
        mesh=mesh,
        in_specs=(split,) * 4 + (P(), P()),
        out_specs=(split,) * 4,
        check_vma=False,
    )
```

time: 77.3 us -> 53.4 us (0.69)
  the two profiles are of different devices: /device:TPU:25 before, /device:TPU:454 now
where the time goes in v2:
time: 53.4 us; the launch traced here: 53.2 us
  Pallas kernels  51.4 us (96%)
  between operations  1.3 us (2%)
    pallas_call x1, Pallas kernels, run(): pl.pallas_call(functools.partial(fused_kernel, n, rest, alone, tc, hc, sl...  47 us
    pallas_call x1, Pallas kernels, on_device(): pl.pallas_call(functools.partial(pack_kernel, heads, width), out_shape=(j...  2.32 us
    pallas_call x1, Pallas kernels, on_device(): pl.pallas_call(functools.partial(spread_kernel, heads, width), out_shape=...  2.08 us

profile of v2, /device:TPU:454, one launch (start us, length us, event | category | flops | bytes accessed | tf_op | source)
XLA Modules:
  0.0 53.2 jit_solution(7839228019608072899)
XLA Ops:
  0.6 2.3 %pack.1 = (bf16[4,12,128,128]{3,2,1,0:T(8,128)(2,1)S(1)}, f32[12,27]{1,0:T(8,128)S(1)}, s32[12]{0:T(128)}, s32[1]{0:T(128)}) custom-call(s32[3,12]{1,0:T(4,128)} %bitcast.14, s32[12,27]{1,0:T(8,128)} %mask.1, bf16[128,1536]{1,0:T(8,128)(2,1)} %bitcast.10, bf16[128,1536]{1,0:T(8,128)(2,1)} %bitcast.11, bf16[128,1536]{1,0:T(8,128)(2,1)} %bitcast.12, ...), custom_call_target="tpu_custom_call" | custom-call | tf_op jit(solution)/shard_map/pack/pallas_call | solution.py:484
  3.6 47.5 %conditional.1 = ((bf16[12,128,128]{2,1,0:T(8,128)(2,1)S(1)}, bf16[12,128,128]{2,1,0:T(8,128)(2,1)S(1)}, bf16[12,128,128]{2,1,0:T(8,128)(2,1)S(1)}, bf16[12,128,128]{2,1,0:T(8,128)(2,1)S(1)})) conditional(s32[]{:T(128)} %bitcast.5, (f32[12,27]{1,0:T(8,128)S(1)}, bf16[4,12,128,128]{3,2,1,0:T(8,128)(2,1)S(1)}) %tuple.23, ...), branch_computations={%region_0.0_spmd, %region_1.0_spmd, %region_2.0_spmd, %region_3.0_... | conditional | bytes 8 | solution.py:496
  3.6 47.0 %tiles_3.1 = (bf16[12,128,128]{2,1,0:T(8,128)(2,1)S(1)}, bf16[12,128,128]{2,1,0:T(8,128)(2,1)S(1)}, bf16[12,128,128]{2,1,0:T(8,128)(2,1)S(1)}, bf16[12,128,128]{2,1,0:T(8,128)(2,1)S(1)}) custom-call(f32[12,27]{1,0:T(8,128)S(1)} %get-tuple-element.24.penalty, bf16[4,12,128,128]{3,2,1,0:T(8,128)(2,1)S(1)} %get-tuple-element.25.own), custom_call_target="tpu_custom_call" | custom-call | tf_op jit(solution)/shard_map/cond/branch_2_fun/tiles_3/pallas_call | solution.py:458
  51.2 2.1 %spread.1 = (bf16[128,1536]{1,0:T(8,128)(2,1)}, bf16[128,1536]{1,0:T(8,128)(2,1)}, bf16[128,1536]{1,0:T(8,128)(2,1)}, bf16[128,1536]{1,0:T(8,128)(2,1)}) custom-call(s32[12]{0:T(128)} %get-tuple-element.46.slots, bf16[12,128,128]{2,1,0:T(8,128)(2,1)S(1)} %get-tuple-element.50.o_in, bf16[12,128,128]{2,1,0:T(8,128)(2,1)S(1)} %get-tuple-element.51.dq_in, ...), custom_call_target="tpu_custom_call" | custom-call | tf_op jit(solution)/shard_map/spread/pallas_call | solution.py:498

commit v3 on v2

v3 whole, which is shorter than its diff:
```python
import functools
import math

import jax
import jax.numpy as jnp
from jax import lax
from jax.experimental import pallas as pl
from jax.experimental.pallas import tpu as pltpu
from jax.sharding import PartitionSpec as P

TILE = 32
NEG = -1e30
K, V, Q, G = 0, 1, 2, 3
MESH = pl.DeviceIdType.MESH
LOG2E = 1.0 / math.log(2.0)


def dot_nt(a, b):
    return lax.dot_general(a, b, (((1,), (1,)), ((), ())), preferred_element_type=jnp.float32)


def dot_nn(a, b):
    return lax.dot_general(a, b, (((1,), (0,)), ((), ())), preferred_element_type=jnp.float32)


def fused_kernel(
    n, rest, tc, hc, slab, width,
    penalty, own, own_h,
    o_out, dq_out, dk_out, dv_out,
    xb, xt, xh, stats_col, stats, stats_in,
    lsend, esend, zsend, tsend, trecv, hsend, hrecv, dsend, drecv, ssend, srecv,
):
    scale = 1.0 / math.sqrt(width)
    half = n + rest
    t = lax.axis_index("tm")
    h = lax.axis_index("height")
    t_near = (jnp.maximum(t - 1, 0), jnp.minimum(t + 1, tc - 1))
    h_near = (jnp.maximum(h - 1, 0), jnp.minimum(h + 1, hc - 1))
    has_t = (t > 0, t < tc - 1)
    has_h = (h > 0, h < hc - 1)
    centre = [(0, 0)]
    h_line = [(0, -1), (0, 1)]
    t_line = [(0, 0), (-1, 0), (1, 0)]
    square = h_line + t_line + [(-1, -1), (-1, 1), (1, -1), (1, 1)]
    at = {x: i for i, x in enumerate(square)}
    around = [x for x in square if x != (0, 0)]

    def inside(dt, dr):
        ok = True
        if dt:
            ok = has_t[(dt + 1) // 2]
        if dr:
            ok = jnp.logical_and(ok, has_h[(dr + 1) // 2])
        return ok

    def when(ok, body):
        if ok is True:
            body()
        else:
            pl.when(ok)(body)

    cross = {-1: h == hc // 2, 1: h == hc // 2 - 1}
    outer = jnp.logical_or(t == 0, t == tc - 1)
    inner = {-1: t == 1, 1: t == tc - 2}
    near_end = jnp.logical_or(inner[-1], inner[1])

    def both_of(a, b):
        return b if a is True else jnp.logical_and(a, b)

    barrier = pltpu.get_barrier_semaphore()
    for dt, dr in around:
        def greet(dt=dt, dr=dr):
            pl.semaphore_signal(barrier, inc=1, device_id=(t + dt, h + dr), device_id_type=MESH)
        when(inside(dt, dr), greet)

    local = []
    if n:
        local.append(pltpu.make_async_copy(own.at[:, pl.ds(0, n)], xb.at[:, :, at[0, 0]], lsend.at[0]))
    if rest:
        local.append(pltpu.make_async_copy(own.at[:, pl.ds(n, rest)], xt.at[:, :, 0], lsend.at[1]))
    for copy in local:
        copy.start()

    fill = []
    for dt, dr in around:
        def add(source, target, number, dt=dt, dr=dr):
            copy = pltpu.make_async_copy(source, target, esend.at[number])
            fill.append((jnp.logical_not(inside(dt, dr)), copy))
        if n:
            add(own.at[:, pl.ds(0, n)], xb.at[:, :, at[dt, dr]], at[dt, dr])
        if rest and dr == 0:
            add(own.at[:, pl.ds(n, rest)], xt.at[:, :, t_line.index((dt, 0))], 10 + dt)
        if rest and dt == 0:
            add(own.at[:, pl.ds(half, rest)], xh.at[:, :, h_line.index((0, dr))], 13 + dr)

        def clear(dt=dt, dr=dr):
            stats_in[dt + 1, dr + 1] = jnp.zeros(stats_in.shape[2:], jnp.float32)
        when(jnp.logical_not(inside(dt, dr)), clear)
    for ok, copy in fill:
        when(ok, copy.start)
    stats_col[...] = jnp.zeros((slab, slab), jnp.float32)

    count_t = has_t[0].astype(jnp.int32) + has_t[1].astype(jnp.int32)
    count_h = has_h[0].astype(jnp.int32) + has_h[1].astype(jnp.int32)
    pl.semaphore_wait(barrier, count_t + count_h + count_t * count_h)

    def t_copy(array, part, d):
        if part == 0:
            source, target = own.at[array, pl.ds(0, n)], xb.at[array, :, at[-d, 0]]
        else:
            source, target = own.at[array, pl.ds(n, rest)], xt.at[array, :, t_line.index((-d, 0))]
        return pltpu.make_async_remote_copy(
            src_ref=source, dst_ref=target,
            send_sem=tsend.at[array, part, d + 1], recv_sem=trecv.at[array, part, 1 - d],
            device_id=(t_near[(d + 1) // 2], h), device_id_type=MESH,
        )

    def h_copy(array, part, d):
        if part == 0:
            source, target = own_h.at[array, pl.ds(0, n)], xb.at[array, :, at[0, -d]]
        else:
            source, target = own_h.at[array, pl.ds(n, rest)], xh.at[array, :, h_line.index((0, -d))]
        return pltpu.make_async_remote_copy(
            src_ref=source, dst_ref=target,
            send_sem=hsend.at[array, part, d + 1], recv_sem=hrecv.at[array, part, 1 - d],
            device_id=(t, h_near[(d + 1) // 2]), device_id_type=MESH,
        )

    def d_copy(array, e, d):
        return pltpu.make_async_remote_copy(
            src_ref=xb.at[array, :, at[e, 0]], dst_ref=xb.at[array, :, at[e, -d]],
            send_sem=dsend.at[array, e + 1, d + 1], recv_sem=drecv.at[array, e + 1, 1 - d],
            device_id=(t, h_near[(d + 1) // 2]), device_id_type=MESH,
        )

    def z_copy(array, f, d):
        return pltpu.make_async_remote_copy(
            src_ref=xb.at[array, :, at[0, d]], dst_ref=xb.at[array, :, at[-f, d]],
            send_sem=zsend.at[array], recv_sem=drecv.at[array, 1 - f, d + 1],
            device_id=(t_near[(f + 1) // 2], h), device_id_type=MESH,
        )

    def s_copy(group, dt, dr):
        return pltpu.make_async_remote_copy(
            src_ref=stats.at[group], dst_ref=stats_in.at[1 - dt, 1 - dr, group],
            send_sem=ssend.at[group, dt + 1, dr + 1], recv_sem=srecv.at[group, 1 - dt, 1 - dr],
            device_id=(t_near[(dt + 1) // 2] if dt else t, h_near[(dr + 1) // 2] if dr else h),
            device_id_type=MESH,
        )

    both, lone = n > 0, rest > 0

    def t_start(array, part):
        for d in (-1, 1):
            when(inside(d, 0), lambda d=d: t_copy(array, part, d).start())

    def h_start(array, part, ok=True):
        for d in (-1, 1):
            when(both_of(ok, inside(0, d)), lambda d=d: h_copy(array, part, d).start())

    def t_wait(array, part):
        for e in (-1, 1):
            when(inside(e, 0), lambda e=e: t_copy(array, part, -e).wait_recv())

    def h_wait(array, part):
        for e in (-1, 1):
            ok = inside(0, e)
            if part == 0:
                ok = both_of(ok, jnp.logical_not(jnp.logical_and(near_end, cross[e])))
            when(ok, lambda e=e: h_copy(array, part, -e).wait_recv())

    def z_relay(array):
        for d in (-1, 1):
            for f in (-1, 1):
                def forward(d=d, f=f):
                    h_copy(array, 0, -d).wait_recv()
                    z_copy(array, f, d).start()
                when(jnp.logical_and(inner[f], cross[d]), forward)

    def relay(array):
        for e in (-1, 1):
            def forward(e=e):
                t_copy(array, 0, -e).wait_recv()
                for d in (-1, 1):
                    ok = jnp.logical_and(inside(0, d), jnp.logical_not(jnp.logical_and(outer, cross[d])))
                    when(ok, lambda d=d: d_copy(array, e, d).start())
            when(inside(e, 0), forward)

    def d_wait(array):
        for e in (-1, 1):
            for d in (-1, 1):
                when(inside(e, d), lambda e=e, d=d: d_copy(array, e, -d).wait_recv())

    def s_start(group, steps):
        for dt, dr in steps:
            when(inside(dt, dr), lambda dt=dt, dr=dr: s_copy(group, dt, dr).start())

    def s_wait(group, steps):
        for dt, dr in steps:
            when(inside(dt, dr), lambda dt=dt, dr=dr: s_copy(group, -dt, -dr).wait_recv())

    row_tile = lax.broadcasted_iota(jnp.int32, (slab, slab), 0) // TILE
    col_tile = lax.broadcasted_iota(jnp.int32, (slab, slab), 1) // TILE
    step = col_tile - row_tile
    lane = lax.broadcasted_iota(jnp.int32, (slab, slab), 1)

    def added(slot, dt, dr, sign, minus=None):
        first = 9 * (sign * dt + 1) + 3 * (sign * dr + 1) + 1
        total = jnp.full((slab, slab), NEG, jnp.float32)
        for dw in (-1, 0, 1):
            value = penalty[slot, first + dw]
            if dt or dr:
                value = jnp.where(inside(dt, dr), value, NEG)
            if minus is not None:
                value = value - minus
            total = jnp.where(step == sign * dw, value, total)
        return total

    def joined(pieces):
        return pieces[0] if len(pieces) == 1 else jnp.concatenate(pieces, axis=1)

    def weighted(rows, segments, array):
        total, start = None, 0
        for blocks, get in segments:
            size = len(blocks) * slab
            part = dot_nn(rows[:, start : start + size], get(array))
            total = part if total is None else total + part
            start += size
        return total

    def first_pass(slot, segments):
        query, cot = own[Q, slot], own[G, slot]
        scores = joined([dot_nt(query, get(K)) for _, get in segments]) * (scale * LOG2E)
        scores = scores + joined([added(slot, dt, dr, 1) for blocks, _ in segments for dt, dr in blocks])
        highest = jnp.max(scores, axis=1, keepdims=True)
        weights = jnp.exp2(scores - highest)
        total = jnp.sum(weights, axis=1, keepdims=True)
        inverse = 1.0 / total
        out = (weighted(weights.astype(jnp.bfloat16), segments, V) * inverse).astype(jnp.bfloat16)
        o_out[slot] = out
        delta = jnp.sum(cot.astype(jnp.float32) * out.astype(jnp.float32), axis=1, keepdims=True)
        slope = joined([dot_nt(cot, get(V)) for _, get in segments])
        slope = (weights * (slope - delta)).astype(jnp.bfloat16)
        dq_out[slot] = (weighted(slope, segments, K) * (inverse * scale)).astype(jnp.bfloat16)
        log_sum = highest + jnp.log2(total)
        held = jnp.where(lane == slot, log_sum, stats_col[...])
        stats_col[...] = jnp.where(lane == slot + 16, delta, held)

    def second_pass(group, slot, segments):
        key, value = own[K, slot], own[V, slot]
        scores = joined([dot_nt(key, get(Q)) for _, get in segments]) * (scale * LOG2E)
        shifts, deltas = [], []
        for blocks, _ in segments:
            for dt, dr in blocks:
                source = stats_in.at[dt + 1, dr + 1, group] if dt or dr else stats.at[group]
                shifts.append(added(slot, dt, dr, -1, source[pl.ds(slot, 1), :]))
                deltas.append(source[pl.ds(slot + 16, 1), :])
        probs = jnp.exp2(scores + joined(shifts))
        dv_out[slot] = weighted(probs.astype(jnp.bfloat16), segments, G).astype(jnp.bfloat16)
        slope = joined([dot_nt(value, get(G)) for _, get in segments]) - joined(deltas)
        slope = (probs * slope).astype(jnp.bfloat16)
        dk_out[slot] = (weighted(slope, segments, Q) * scale).astype(jnp.bfloat16)

    def loop(count, body):
        if n + rest == count or rest:
            for i in range(count):
                body(i)
        elif count:
            lax.fori_loop(0, count, lambda i, c: (body(i), c)[1], 0)

    def slabs(ref, i, size):
        return lambda array: ref[array, i, :size].reshape(size * slab, width)

    def nine(i):
        return [(square, slabs(xb, i, 9))]

    def over_time(i):
        return [(t_line, slabs(xt, i, 3))]

    def over_height(slot, ref, i):
        return [(h_line, slabs(ref, i, 2)), (centre, lambda array: own[array, slot])]

    def take_stats(group):
        stats[group] = jnp.transpose(stats_col[...])[: stats.shape[1]]

    sides = [(-1, 0), (1, 0)]
    for array in range(4):
        t_start(array, 0)
        if array < 2:
            h_start(array, 0)
    if lone:
        for array in (K, V):
            t_start(array, 1)
            h_start(array, 1)
    for copy in local:
        copy.wait()
    for ok, copy in fill:
        when(ok, copy.wait)
    relay(K)
    relay(V)
    h_start(Q, 0)
    h_start(G, 0)
    z_relay(K)
    z_relay(V)
    h_wait(K, 0)
    h_wait(V, 0)
    loop(n, lambda i: first_pass(half + i, over_height(half + i, xb, i)))
    relay(Q)
    z_relay(Q)
    if lone:
        h_wait(K, 1)
        h_wait(V, 1)
        loop(rest, lambda i: first_pass(half + n + i, over_height(half + n + i, xh, i)))
    slow = jnp.logical_and(outer, jnp.logical_or(cross[-1], cross[1]))
    if lone:
        for array in (Q, G):
            h_start(array, 1, slow)
    d_wait(K)
    d_wait(V)
    loop(n, lambda i: first_pass(i, nine(i)))
    take_stats(0)
    s_start(0, around)
    relay(G)
    z_relay(G)
    if lone:
        for array in (Q, G):
            t_start(array, 1)
            h_start(array, 1, jnp.logical_not(slow))
        t_wait(K, 1)
        t_wait(V, 1)
        loop(rest, lambda i: first_pass(n + i, over_time(i)))
        take_stats(1)
    s_wait(0, around)
    if lone:
        s_start(1, sides)
    h_wait(Q, 0)
    h_wait(G, 0)
    loop(n, lambda i: second_pass(0, half + i, over_height(half + i, xb, i)))
    d_wait(Q)
    d_wait(G)
    loop(n, lambda i: second_pass(0, i, nine(i)))
    if lone:
        h_wait(Q, 1)
        h_wait(G, 1)
        loop(rest, lambda i: second_pass(0, half + n + i, over_height(half + n + i, xh, i)))
        t_wait(Q, 1)
        t_wait(G, 1)
        s_wait(1, sides)
        loop(rest, lambda i: second_pass(1, n + i, over_time(i)))

    for array in range(4):
        for part in ([0] if both else []) + ([1] if lone else []):
            for d in (-1, 1):
                when(inside(d, 0), lambda array=array, part=part, d=d: t_copy(array, part, d).wait_send())
                when(inside(0, d), lambda array=array, part=part, d=d: h_copy(array, part, d).wait_send())
        if both:
            for e in (-1, 1):
                for d in (-1, 1):
                    ok = jnp.logical_and(inside(e, d), jnp.logical_not(jnp.logical_and(outer, cross[d])))
                    when(ok, lambda array=array, e=e, d=d: d_copy(array, e, d).wait_send())
            for d in (-1, 1):
                for f in (-1, 1):
                    when(jnp.logical_and(inner[f], cross[d]), z_copy(array, f, d).wait_send)
    for dt, dr in around:
        when(inside(dt, dr), lambda dt=dt, dr=dr: s_copy(0, dt, dr).wait_send())
    if lone:
        for d in (-1, 1):
            when(inside(d, 0), lambda d=d: s_copy(1, d, 0).wait_send())


def pack_kernel(
    heads, width, most, window, mask, k_in, v_in, q_in, g_in, packed, packed_h, penalty, slots, kind_out
):
    half = heads // 2
    time = [window[0, i] for i in range(heads)]
    height = [window[1, i] for i in range(heads)]
    total = functools.reduce(lambda x, y: x + y, [x * y for x, y in zip(time, height)])
    kind_out[0] = jnp.where(total > most, 1, 0)
    place = lax.broadcasted_iota(jnp.int32, (1, 27), 1)
    moved = (place // 9 != 1, place // 3 % 3 != 1, place % 3 != 1)
    seen = [0, total, half + total, half]
    for i in range(heads):
        both = time[i] * height[i]
        kinds = [both, time[i] - both, height[i] - both, 1 - time[i] - height[i] + both]
        slot = sum(k * c for k, c in zip(kinds, seen))
        slot_h = jnp.where(height[i] == 1, jnp.where(time[i] == 1, seen[0], seen[2] - half), half)
        seen = [c + k for k, c in zip(kinds, seen)]
        slots[i] = slot
        for number, ref in ((K, k_in), (V, v_in), (Q, q_in), (G, g_in)):
            value = ref[:, i * width : (i + 1) * width]
            packed[number, slot] = value
            packed_h[number, slot_h] = value
        row = jnp.where(mask[i : i + 1, :] == 1, 0.0, NEG)
        for axis in range(3):
            row = jnp.where(moved[axis], row + jnp.where(window[axis, i] == 1, 0.0, NEG), row)
        penalty[pl.ds(slot, 1), :] = row


def spread_kernel(heads, width, slots, o_in, dq_in, dk_in, dv_in, o_out, dq_out, dk_out, dv_out):
    for source, target in ((o_in, o_out), (dq_in, dq_out), (dk_in, dk_out), (dv_in, dv_out)):
        for i in range(heads):
            target[:, i * width : (i + 1) * width] = source[slots[i]]


def on_device(tc, hc, query_vecs, key_vecs, value_vecs, grad_output, tile_window, neighbour_mask):
    slab, features = query_vecs.shape[2:]
    heads = tile_window.shape[0]
    half = heads // 2
    width = features // heads
    vmem = pl.BlockSpec(memory_space=pltpu.VMEM)
    smem = pl.BlockSpec(memory_space=pltpu.SMEM)
    packed = jax.ShapeDtypeStruct((heads, slab, width), jnp.bfloat16)
    dma = pltpu.SemaphoreType.DMA

    def branch(number, n):
        rest = half - n

        def run(penalty, own, own_h):
            return pl.pallas_call(
                functools.partial(fused_kernel, n, rest, tc, hc, slab, width),
                out_shape=(packed,) * 4,
                in_specs=[smem, vmem, vmem],
                out_specs=(vmem,) * 4,
                scratch_shapes=[
                    pltpu.VMEM((4, n, 9, slab, width), jnp.bfloat16),
                    pltpu.VMEM((4, max(rest, 1), 3, slab, width), jnp.bfloat16),
                    pltpu.VMEM((4, max(rest, 1), 2, slab, width), jnp.bfloat16),
                    pltpu.VMEM((slab, slab), jnp.float32),
                    pltpu.VMEM((2, 32, slab), jnp.float32),
                    pltpu.VMEM((3, 3, 2, 32, slab), jnp.float32),
                    dma((3,)), dma((15,)), dma((4,)),
                    dma((4, 2, 3)), dma((4, 2, 3)),
                    dma((4, 2, 3)), dma((4, 2, 3)),
                    dma((4, 3, 3)), dma((4, 3, 3)),
                    dma((2, 3, 3)), dma((2, 3, 3)),
                ],
                compiler_params=pltpu.CompilerParams(
                    collective_id=number, has_side_effects=True, vmem_limit_bytes=40 * 1024 * 1024
                ),
                name=f"tiles_{n}",
            )(penalty, own, own_h)
        return run

    arrays = [x.reshape(slab, features) for x in (key_vecs, value_vecs, query_vecs, grad_output)]
    most = 2 * half // 3
    own, own_h, penalty, slots, joint = pl.pallas_call(
        functools.partial(pack_kernel, heads, width, most),
        out_shape=(
            jax.ShapeDtypeStruct((4, heads, slab, width), jnp.bfloat16),
            jax.ShapeDtypeStruct((4, half + 1, slab, width), jnp.bfloat16),
            jax.ShapeDtypeStruct((heads, 27), jnp.float32),
            jax.ShapeDtypeStruct((heads,), jnp.int32),
            jax.ShapeDtypeStruct((1,), jnp.int32),
        ),
        in_specs=[smem, vmem] + [vmem] * 4,
        out_specs=(vmem, vmem, vmem, smem, smem),
        name="pack",
    )(tile_window.T, neighbour_mask, *arrays)
    results = lax.switch(joint[0], [branch(0, most), branch(1, half)], penalty, own, own_h)
    flat = jax.ShapeDtypeStruct((slab, features), jnp.bfloat16)
    outs = pl.pallas_call(
        functools.partial(spread_kernel, heads, width),
        out_shape=(flat,) * 4,
        in_specs=[smem] + [vmem] * 4,
        out_specs=(vmem,) * 4,
        name="spread",
    )(slots, *results)
    return tuple(x.reshape(1, 1, slab, features) for x in outs)


def solution(mesh):
    split = P("tm", "height", None, None)
    return jax.shard_map(
        functools.partial(on_device, mesh.shape["tm"], mesh.shape["height"]),
        mesh=mesh,
        in_specs=(split,) * 4 + (P(), P()),
        out_specs=(split,) * 4,
        check_vma=False,
    )
```

time: 53.4 us -> 55.3 us (1.036)
  Pallas kernels: 51.4 us -> 53.6 us
    pallas_call x2, Pallas kernels: 49.4 us -> 51 us  [the longest x1 48.6 us: run(): pl.pallas_call(functools.partial(fused_kernel, n, rest, tc, hc, slab, wid...]
where the time goes in v3:
time: 55.3 us; the launch traced here: 55.1 us
  Pallas kernels  53.6 us (97%)
  between operations  1.3 us (2%)
    pallas_call x1, Pallas kernels, run(): pl.pallas_call(functools.partial(fused_kernel, n, rest, tc, hc, slab, wid...  48.6 us
    pallas_call x1, Pallas kernels, on_device(): pl.pallas_call(functools.partial(spread_kernel, heads, width), out_shape=...  2.54 us
    pallas_call x1, Pallas kernels, on_device(): pl.pallas_call(functools.partial(pack_kernel, heads, width, most), out_sh...  2.43 us

profile of v3, /device:TPU:454, one launch (start us, length us, event | category | flops | bytes accessed | tf_op | source)
XLA Modules:
  0.0 55.1 jit_solution(18203794236868259992)
XLA Ops:
  0.6 2.4 %pack.1 = (bf16[4,12,128,128]{3,2,1,0:T(8,128)(2,1)S(1)}, bf16[4,7,128,128]{3,2,1,0:T(8,128)(2,1)S(1)}, f32[12,27]{1,0:T(8,128)S(1)}, s32[12]{0:T(128)}, s32[1]{0:T(128)}) custom-call(s32[3,12]{1,0:T(4,128)} %bitcast.14, s32[12,27]{1,0:T(8,128)} %mask.1, bf16[128,1536]{1,0:T(8,128)(2,1)} %bitcast.10, bf16[128,1536]{1,0:T(8,128)(2,1)} %bitcast.11, ...), custom_call_target="tpu_custom_call" | custom-call | tf_op jit(solution)/shard_map/pack/pallas_call | solution.py:446
  3.7 48.9 %conditional.1 = ((bf16[12,128,128]{2,1,0:T(8,128)(2,1)S(1)}, bf16[12,128,128]{2,1,0:T(8,128)(2,1)S(1)}, bf16[12,128,128]{2,1,0:T(8,128)(2,1)}, bf16[12,128,128]{2,1,0:T(8,128)(2,1)})) conditional(s32[]{:T(128)} %bitcast.5, (f32[12,27]{1,0:T(8,128)S(1)}, bf16[4,12,128,128]{3,2,1,0:T(8,128)(2,1)S(1)}, ...), branch_computations={%region_0.0_spmd, %region_1.0_spmd} | conditional | bytes 8 | solution.py:459
  3.7 48.6 %tiles_4.1 = (bf16[12,128,128]{2,1,0:T(8,128)(2,1)S(1)}, bf16[12,128,128]{2,1,0:T(8,128)(2,1)S(1)}, bf16[12,128,128]{2,1,0:T(8,128)(2,1)}, bf16[12,128,128]{2,1,0:T(8,128)(2,1)}) custom-call(f32[12,27]{1,0:T(8,128)S(1)} %get-tuple-element.12.penalty, bf16[4,12,128,128]{3,2,1,0:T(8,128)(2,1)S(1)} %get-tuple-element.13.own, ...), custom_call_target="tpu_custom_call" | custom-call | tf_op jit(solution)/shard_map/cond/branch_0_fun/tiles_4/pallas_call | solution.py:419
  52.6 2.5 %spread.1 = (bf16[128,1536]{1,0:T(8,128)(2,1)}, bf16[128,1536]{1,0:T(8,128)(2,1)}, bf16[128,1536]{1,0:T(8,128)(2,1)}, bf16[128,1536]{1,0:T(8,128)(2,1)}) custom-call(s32[12]{0:T(128)} %get-tuple-element.35.slots, bf16[12,128,128]{2,1,0:T(8,128)(2,1)S(1)} %get-tuple-element.40.o_in, bf16[12,128,128]{2,1,0:T(8,128)(2,1)S(1)} %get-tuple-element.41.dq_in, ...), custom_call_target="tpu_custom_call" | custom-call | tf_op jit(solution)/shard_map/spread/pallas_call | solution.py:461

commit v4 on v3

--- a/solution.py
+++ b/solution.py
@@ -64,6 +64,8 @@
     inner = {-1: t == 1, 1: t == tc - 2}
     near_end = jnp.logical_or(inner[-1], inner[1])
 
+    held = jnp.logical_and(t == tc // 2, jnp.logical_and(h >= hc // 2 - 2, h < hc // 2 + 2))
+
     def both_of(a, b):
         return b if a is True else jnp.logical_and(a, b)
 
@@ -150,13 +152,19 @@
 
     both, lone = n > 0, rest > 0
 
-    def t_start(array, part):
+    def t_start(array, part, ok=True, late=None):
         for d in (-1, 1):
-            when(inside(d, 0), lambda d=d: t_copy(array, part, d).start())
-
-    def h_start(array, part, ok=True):
+            go = both_of(ok, inside(d, 0))
+            if late is not None and d == -1:
+                go = jnp.logical_and(go, held if late else jnp.logical_not(held))
+            if not late or d == -1:
+                when(go, lambda d=d: t_copy(array, part, d).start())
+
+    def h_start(array, part, early=False):
         for d in (-1, 1):
-            when(both_of(ok, inside(0, d)), lambda d=d: h_copy(array, part, d).start())
+            shared = jnp.logical_and(outer, cross[d])
+            ok = shared if early else jnp.logical_and(inside(0, d), jnp.logical_not(shared))
+            when(ok, lambda d=d: h_copy(array, part, d).start())
 
     def t_wait(array, part):
         for e in (-1, 1):
@@ -177,14 +185,14 @@
                     z_copy(array, f, d).start()
                 when(jnp.logical_and(inner[f], cross[d]), forward)
 
-    def relay(array):
+    def relay(array, here=True):
         for e in (-1, 1):
             def forward(e=e):
                 t_copy(array, 0, -e).wait_recv()
                 for d in (-1, 1):
                     ok = jnp.logical_and(inside(0, d), jnp.logical_not(jnp.logical_and(outer, cross[d])))
                     when(ok, lambda d=d: d_copy(array, e, d).start())
-            when(inside(e, 0), forward)
+            when(both_of(here, inside(e, 0)), forward)
 
     def d_wait(array):
         for e in (-1, 1):
@@ -284,13 +292,19 @@
         stats[group] = jnp.transpose(stats_col[...])[: stats.shape[1]]
 
     sides = [(-1, 0), (1, 0)]
+    slow = jnp.logical_and(outer, jnp.logical_or(cross[-1], cross[1]))
+    prompt = jnp.logical_not(slow)
+    for arrays in ((K, V), (Q, G)):
+        for part in (0, 1) if lone else (0,):
+            for array in arrays:
+                h_start(array, part, True)
     for array in range(4):
-        t_start(array, 0)
+        t_start(array, 0, late=None if array < 2 else False)
         if array < 2:
             h_start(array, 0)
     if lone:
         for array in (K, V):
-            t_start(array, 1)
+            t_start(array, 1, late=False)
             h_start(array, 1)
     for copy in local:
         copy.wait()
@@ -300,32 +314,38 @@
     relay(V)
     h_start(Q, 0)
     h_start(G, 0)
+    if lone:
+        for array in (Q, G):
+            t_start(array, 1, slow)
+    relay(Q, slow)
+    relay(G, slow)
     z_relay(K)
     z_relay(V)
     h_wait(K, 0)
     h_wait(V, 0)
     loop(n, lambda i: first_pass(half + i, over_height(half + i, xb, i)))
-    relay(Q)
+    t_start(Q, 0, late=True)
+    t_start(G, 0, late=True)
+    if lone:
+        t_start(K, 1, late=True)
+        t_start(V, 1, late=True)
+    relay(Q, prompt)
     z_relay(Q)
     if lone:
         h_wait(K, 1)
         h_wait(V, 1)
         loop(rest, lambda i: first_pass(half + n + i, over_height(half + n + i, xh, i)))
-    slow = jnp.logical_and(outer, jnp.logical_or(cross[-1], cross[1]))
-    if lone:
-        for array in (Q, G):
-            h_start(array, 1, slow)
     d_wait(K)
     d_wait(V)
     loop(n, lambda i: first_pass(i, nine(i)))
     take_stats(0)
     s_start(0, around)
-    relay(G)
+    relay(G, prompt)
     z_relay(G)
     if lone:
         for array in (Q, G):
-            t_start(array, 1)
-            h_start(array, 1, jnp.logical_not(slow))
+            t_start(array, 1, prompt)
+            h_start(array, 1)
         t_wait(K, 1)
         t_wait(V, 1)
         loop(rest, lambda i: first_pass(n + i, over_time(i)))

time: 55.3 us -> 55.2 us (level)
  no operation moved by 1% of the time
where the time goes in v4:
time: 55.2 us; the launch traced here: 55 us
  Pallas kernels  53.5 us (97%)
  between operations  1.3 us (2%)
    pallas_call x1, Pallas kernels, run(): pl.pallas_call(functools.partial(fused_kernel, n, rest, tc, hc, slab, wid...  48.5 us
    pallas_call x1, Pallas kernels, on_device(): pl.pallas_call(functools.partial(spread_kernel, heads, width), out_shape=...  2.54 us
    pallas_call x1, Pallas kernels, on_device(): pl.pallas_call(functools.partial(pack_kernel, heads, width, most), out_sh...  2.43 us

profile of v4, /device:TPU:454, one launch (start us, length us, event | category | flops | bytes accessed | tf_op | source)
XLA Modules:
  0.0 55.0 jit_solution(15204161757854193639)
XLA Ops:
  0.6 2.4 %pack.1 = (bf16[4,12,128,128]{3,2,1,0:T(8,128)(2,1)S(1)}, bf16[4,7,128,128]{3,2,1,0:T(8,128)(2,1)S(1)}, f32[12,27]{1,0:T(8,128)S(1)}, s32[12]{0:T(128)}, s32[1]{0:T(128)}) custom-call(s32[3,12]{1,0:T(4,128)} %bitcast.14, s32[12,27]{1,0:T(8,128)} %mask.1, bf16[128,1536]{1,0:T(8,128)(2,1)} %bitcast.10, bf16[128,1536]{1,0:T(8,128)(2,1)} %bitcast.11, ...), custom_call_target="tpu_custom_call" | custom-call | tf_op jit(solution)/shard_map/pack/pallas_call | solution.py:466
  3.7 48.8 %conditional.1 = ((bf16[12,128,128]{2,1,0:T(8,128)(2,1)S(1)}, bf16[12,128,128]{2,1,0:T(8,128)(2,1)S(1)}, bf16[12,128,128]{2,1,0:T(8,128)(2,1)}, bf16[12,128,128]{2,1,0:T(8,128)(2,1)})) conditional(s32[]{:T(128)} %bitcast.5, (f32[12,27]{1,0:T(8,128)S(1)}, bf16[4,12,128,128]{3,2,1,0:T(8,128)(2,1)S(1)}, ...), branch_computations={%region_0.0_spmd, %region_1.0_spmd} | conditional | bytes 8 | solution.py:479
  3.7 48.5 %tiles_4.1 = (bf16[12,128,128]{2,1,0:T(8,128)(2,1)S(1)}, bf16[12,128,128]{2,1,0:T(8,128)(2,1)S(1)}, bf16[12,128,128]{2,1,0:T(8,128)(2,1)}, bf16[12,128,128]{2,1,0:T(8,128)(2,1)}) custom-call(f32[12,27]{1,0:T(8,128)S(1)} %get-tuple-element.12.penalty, bf16[4,12,128,128]{3,2,1,0:T(8,128)(2,1)S(1)} %get-tuple-element.13.own, ...), custom_call_target="tpu_custom_call" | custom-call | tf_op jit(solution)/shard_map/cond/branch_0_fun/tiles_4/pallas_call | solution.py:439
  52.5 2.5 %spread.1 = (bf16[128,1536]{1,0:T(8,128)(2,1)}, bf16[128,1536]{1,0:T(8,128)(2,1)}, bf16[128,1536]{1,0:T(8,128)(2,1)}, bf16[128,1536]{1,0:T(8,128)(2,1)}) custom-call(s32[12]{0:T(128)} %get-tuple-element.35.slots, bf16[12,128,128]{2,1,0:T(8,128)(2,1)S(1)} %get-tuple-element.40.o_in, bf16[12,128,128]{2,1,0:T(8,128)(2,1)S(1)} %get-tuple-element.41.dq_in, ...), custom_call_target="tpu_custom_call" | custom-call | tf_op jit(solution)/shard_map/spread/pallas_call | solution.py:481
